TPU v7x, 32 devices: a whole 2x2x4 slice. The times are simulated.
32 devices in a mesh: seq: 8 (over z, x), head: 4 (over y, core).
Axes of the slice: x: 2, y: 2, z: 4, core: 2. Of those that a mesh axis runs over, the one named last changes fastest.
Arguments:
- tokens_in: bfloat16 [256, 32, 6144], P('seq', None, 'head'), may hold values from -6 to 6
- gate_rows: bfloat16 [256, 32, 6144], P('seq', None, 'head'), may hold values from -28 to 28
- gate_cols: bfloat16 [256, 32, 6144], P(None, 'seq', 'head'), may hold values from -28 to 28
- write_rows: bfloat16 [64, 8192], P(None, 'seq'), may hold values from -6 to 6
- read_rows: bfloat16 [64, 8192], P(None, 'seq'), may hold values from -0.75 to 0.75
- step_rows: float32 [48, 8192], P('head', 'seq'), may hold values from 0 to 2, as said below
- decay_rows: float32 [48, 8192], P('head', 'seq'), may hold values from -1 to 0, as said below
- skip_rows: float32 [48], P('head'), may hold values from 0.5 to 2
- norm_rows: float32 [6144], P('head'), may hold values from 0.5 to 1.5
- write_cols: bfloat16 [64, 8192], P(None, 'seq'), may hold values from -6 to 6
- read_cols: bfloat16 [64, 8192], P(None, 'seq'), may hold values from -0.75 to 0.75
- step_cols: float32 [48, 8192], P('head', 'seq'), may hold values from 0 to 2, as said below
- decay_cols: float32 [48, 8192], P('head', 'seq'), may hold values from -1 to 0, as said below
- skip_cols: float32 [48], P('head'), may hold values from 0.5 to 2
- norm_cols: float32 [6144], P('head'), may hold values from 0.5 to 1.5
Outputs:
- mixed_cols: bfloat16 [256, 32, 6144], P(None, 'seq', 'head')
Inputs may be any that keep to these rules, and one draw needn't show every extreme that they name: `step_rows`: positive. `step_cols`: positive. `decay_rows`: never positive. `decay_cols`: never positive.
All inputs are finite; a program needn't handle non-finite values.
Results may differ from a plain program's by a relative error of at most 0.0063.
Values may be sent and summed in bfloat16 or wider, within the bound.
A program may use at most 128 MiB of HBM per device.

v0:
```python
import functools
import jax
import jax.numpy as jnp
from jax import lax
from jax.experimental import pallas as pl
from jax.experimental.pallas import tpu as pltpu
from jax.sharding import PartitionSpec as P

BLOCK = 256
LANES = 128
EPSILON = 1e-05
LOG2E = 1.4426950408889634
HIGHEST = lax.Precision.HIGHEST
MESH = pl.DeviceIdType.MESH
F32 = jnp.float32
BF16 = jnp.bfloat16
VMEM_BYTES = 60 * 1024 * 1024


def contract(a, b, dims, precision=None):
    return lax.dot_general(
        a, b, (dims, ((), ())), precision=precision, preferred_element_type=F32
    )


def iota(shape, axis):
    return lax.broadcasted_iota(jnp.int32, shape, axis)


def block_sums(decay):
    upper = (iota((BLOCK, BLOCK), 0) <= iota((BLOCK, BLOCK), 1)).astype(F32)
    cumulative = contract(decay, upper, ((1,), (0,)), HIGHEST)
    total = contract(decay, jnp.ones((BLOCK, LANES), F32), ((1,), (0,)), HIGHEST)
    return cumulative, total


def head_state(write32, weight_row, tokens):
    loaded = (write32 * weight_row).astype(BF16)
    return contract(loaded, tokens, ((1,), (0,)))


def column_scale(local_cols, per_col, grid_rows, grid_cols, place_ref, scales):
    high = BLOCK // grid_cols
    column = place_ref[0] * local_cols + pl.program_id(0) // per_col
    shape = (BLOCK, scales.shape[0])
    row = iota(shape, 0)
    depth = scales.shape[0] * grid_rows // BLOCK
    source = (row // grid_rows) * depth + (row % grid_rows) // high
    picked = contract((iota(shape, 1) == source).astype(F32), scales, ((1,), (0,)), HIGHEST)
    lane = (iota((BLOCK, BLOCK), 0) % high) * grid_cols + column
    return jnp.sum(jnp.where(iota((BLOCK, BLOCK), 1) == lane, picked, 0.0), axis=1, keepdims=True)


def states_kernel(heads, scale_of, *refs):
    if scale_of is None:
        x_ref, write_ref, step_ref, decay_ref, end_ref, total_ref = refs
    else:
        (place_ref, scales_ref, gain_ref, x_ref, write_ref, step_ref, decay_ref, end_ref,
         total_ref, hidden_ref) = refs
    step_at = pl.program_id(0)

    @pl.when(step_at == 0)
    def _():
        end_ref[...] = jnp.zeros_like(end_ref)
        total_ref[...] = jnp.zeros_like(total_ref)

    cumulative, total = block_sums(decay_ref[...] * LOG2E)
    tokens = x_ref[...].reshape(BLOCK, x_ref.shape[-1])
    if scale_of is not None:
        scale = scale_of(place_ref, scales_ref[...])
    write32 = write_ref[...].astype(F32)
    final = total[:, :1]
    weights = jnp.exp2(final - cumulative) * step_ref[...]
    fade = jnp.exp2(total)
    for h in range(heads):
        lanes = slice(h * LANES, (h + 1) * LANES)
        own = tokens[:, lanes]
        if scale_of is not None:
            own = (own.astype(F32) * scale * gain_ref[:, lanes]).astype(BF16)
            hidden_ref[0, :, lanes] = own
        gained = head_state(write32, weights[h : h + 1], own)
        end_ref[h] = fade[h : h + 1] * end_ref[h] + gained
    total_ref[...] += total


def main_kernel(
    heads, cols, skip_ref, x_ref, gate_ref, write_ref, read_ref, step_ref, decay_ref, prior_ref,
    gated_ref, squares_ref, state, turned,
):
    @pl.when(pl.program_id(0) == 0)
    def _():
        state[...] = prior_ref[...]
        squares_ref[...] = jnp.zeros_like(squares_ref)

    main_block(
        heads, cols, pl.program_id(0), skip_ref, x_ref, gate_ref, write_ref, read_ref, step_ref,
        decay_ref, gated_ref, squares_ref, state, turned,
    )


def main_block(
    heads, cols, at, skip_ref, x_ref, gate_ref, write_ref, read_ref, step_ref, decay_ref,
    gated_ref, squares_ref, state, turned,
):
    decay = decay_ref[...] * LOG2E
    step = step_ref[...]
    cumulative, total = block_sums(decay)
    lower = (iota((BLOCK, BLOCK), 0) >= iota((BLOCK, BLOCK), 1)).astype(F32)
    across = contract(lower, decay, ((1,), (1,)), HIGHEST)
    lifting = jnp.exp2(across)
    tokens = x_ref[...].reshape(BLOCK, x_ref.shape[-1])
    write = write_ref[...]
    read = read_ref[...]
    write32 = write.astype(F32)
    scores = contract(read, write, ((0,), (0,))) * lower
    weights = jnp.exp2(total[:, :1] - cumulative) * step
    fade = jnp.exp2(total)
    squares = jnp.zeros((BLOCK, LANES), F32)
    read_twice = jnp.concatenate([read, read], axis=0)
    high = BLOCK // cols
    for h in range(heads):
        lanes = slice(h * LANES, (h + 1) * LANES)
        own = tokens[:, lanes]
        spread = jnp.minimum(across[:, h : h + 1] - cumulative[h : h + 1], 0.0)
        mixing = (jnp.exp2(spread) * scores * step[h : h + 1]).astype(BF16)
        held = state[h]
        loaded = (write32 * weights[h : h + 1]).astype(BF16)
        both = contract(jnp.concatenate([mixing, loaded], axis=0), own, ((1,), (0,)))
        out = both[:BLOCK]
        if h % 2 == 0:
            pair = jnp.concatenate([held] + ([state[h + 1]] if h + 1 < heads else []), axis=1)
            coarse = pair.astype(BF16)
            fine = (pair - coarse.astype(F32)).astype(BF16)
            parts = jnp.concatenate([coarse, fine], axis=0)
            from_state = contract(read_twice, parts, ((0,), (0,)))
        side = (h % 2) * LANES
        out += lifting[:, h : h + 1] * from_state[:, side : side + LANES]
        out += skip_ref[h] * own.astype(F32)
        gate = gate_ref[0, :, lanes].astype(F32)
        gated = out * (gate / (1.0 + jnp.exp2(gate * -LOG2E)))
        squares += gated * gated
        if cols > 1:
            near = gated_ref.shape[1]
            slot = turned.at[h % 2]
            slot[...] = gated
            for c in range(cols):
                gated_ref[c // near, c % near, :, lanes] = slot[
                    pl.ds(c, high, stride=cols), :
                ].astype(BF16)
        else:
            gated_ref[0, :, lanes] = gated
        state[h] = fade[h : h + 1] * held + both[BLOCK:]
    row = contract(jnp.ones((8, LANES), F32), squares, ((1,), (1,)), HIGHEST)
    squares_ref[pl.ds(at, 1), :] = row[:1]


def norm_kernel(inner, per_col, gated_ref, squares_ref, gain_ref, out_ref, turned):
    cols, rows, features = gated_ref.shape
    square = (BLOCK, BLOCK)
    start = pl.program_id(0) * rows
    lane = start % BLOCK + iota(square, 0) % rows
    sums = contract((lane == iota(square, 1)).astype(F32), squares_ref[...], ((1,), (1,)), HIGHEST)
    block = (iota(sums.shape, 0) // rows) * per_col + start // BLOCK
    sums = jnp.sum(jnp.where(iota(sums.shape, 1) == block, sums, 0.0), axis=1, keepdims=True)
    scaled = lax.rsqrt(sums / inner + EPSILON)
    for at in range(0, features, LANES):
        lanes = slice(at, at + LANES)
        result = gated_ref[:, :, lanes].reshape(BLOCK, LANES) * scaled * gain_ref[:, lanes]
        if cols > 1:
            slot = turned.at[at // LANES % 2]
            for c in range(cols):
                slot[pl.ds(c, rows, stride=cols), :] = result[c * rows : (c + 1) * rows]
            out_ref[:, :, lanes] = slot[...].reshape(rows, cols, LANES).astype(BF16)
        else:
            out_ref[:, lanes] = result.astype(BF16)


def greet(axes):
    greet_signal(axes)
    greet_wait(axes)


def greet_signal(axes):
    barrier = pltpu.get_barrier_semaphore()
    for axis, count in axes:
        me = lax.axis_index(axis)
        for hop in range(1, count):
            pl.semaphore_signal(
                barrier, inc=1, device_id={axis: lax.rem(me + hop, count)}, device_id_type=MESH
            )


def greet_wait(axes):
    pl.semaphore_wait(
        pltpu.get_barrier_semaphore(), sum(count - 1 for _, count in axes)
    )


def head_sum(count, own_ref, held, send_sems, recv_sems):
    me = lax.axis_index("head")
    copies = []
    for hop in range(1, count):
        copy = pltpu.make_async_remote_copy(
            src_ref=own_ref,
            dst_ref=held.at[hop - 1],
            send_sem=send_sems.at[hop - 1],
            recv_sem=recv_sems.at[hop - 1],
            device_id={"head": lax.rem(me + hop, count)},
            device_id_type=MESH,
        )
        copy.start()
        copies.append(copy)
    for copy in copies:
        copy.wait()
    total = own_ref[...]
    for hop in range(1, count):
        total += held[hop - 1]
    return total


def sum_kernel(count, own_ref, out_ref, held, send_sems, recv_sems):
    greet((("head", count),))
    out_ref[...] = head_sum(count, own_ref, held, send_sems, recv_sems)


def trade_kernel(
    count, head_count, inner, heads, cols, skip_ref, x_hbm, gate_hbm, write_ref, read_ref,
    step_ref, decay_ref, prior_ref, out_ref, scales_ref, x_ref, gate_ref, gated, squares, state,
    turned, held, scale, load_sems, sum_send, sum_recv, scale_send, scale_recv, send_sems,
    recv_sems, local_sems,
):
    axes = (("seq", count), ("head", head_count))
    blocks, features = x_ref.shape[0], x_ref.shape[-1]
    high = gated.shape[3]
    me = lax.axis_index("seq")
    greet_signal(axes)

    def load(b):
        return (
            pltpu.make_async_copy(x_hbm.at[b], x_ref.at[b], load_sems.at[0, b]),
            pltpu.make_async_copy(gate_hbm.at[b], gate_ref.at[b], load_sems.at[1, b]),
        )

    for b in range(blocks):
        for copy in load(b):
            copy.start()
    state[...] = prior_ref[...]
    squares[...] = jnp.zeros_like(squares)

    def compute(b):
        for copy in load(b):
            copy.wait()
        span = pl.ds(pl.multiple_of(b * BLOCK, BLOCK), BLOCK)
        one = pl.ds(b, 1)
        main_block(
            heads, cols, b, skip_ref, x_ref.at[one], gate_ref.at[one], write_ref.at[:, span],
            read_ref.at[:, span], step_ref.at[:, span], decay_ref.at[:, span], gated.at[b],
            squares, state, turned,
        )

    def rows_of(b):
        return out_ref.at[me, :, pl.ds(pl.multiple_of(b * high, high), high)]

    def send(b, ahead):
        to = lax.rem(me + ahead, count)
        return pltpu.make_async_remote_copy(
            src_ref=gated.at[b, to],
            dst_ref=rows_of(b),
            send_sem=send_sems.at[ahead - 1, b],
            recv_sem=recv_sems.at[ahead - 1, b],
            device_id={"seq": to},
            device_id_type=MESH,
        )

    def keep(b):
        return pltpu.make_async_copy(gated.at[b, me], rows_of(b), local_sems.at[b])

    def send_all(b):
        for hop in range(count // 2, count // 2 + count - 1):
            send(b, 1 + (hop - 1) % (count - 1)).start()
        keep(b).start()

    compute(0)
    greet_wait(axes)
    send_all(0)

    def step(b, carry):
        compute(b)
        send_all(b)
        return carry

    lax.fori_loop(1, blocks, step, 0)
    total = head_sum(head_count, squares, held, sum_send, sum_recv)
    scale[...] = lax.rsqrt(total / inner + EPSILON)
    depth = scale.shape[0]
    mine = pl.ds(pl.multiple_of(me * depth, depth), depth)
    copies = []
    for hop in range(1, count):
        copy = pltpu.make_async_remote_copy(
            src_ref=scale,
            dst_ref=scales_ref.at[mine],
            send_sem=scale_send.at[hop - 1],
            recv_sem=scale_recv.at[hop - 1],
            device_id={"seq": lax.rem(me + hop, count)},
            device_id_type=MESH,
        )
        copy.start()
        copies.append(copy)
    scales_ref[mine, :] = scale[...]
    for copy in copies:
        copy.wait()

    def settle(b, carry):
        keep(b).wait()
        for ahead in range(1, count):
            send(b, ahead).wait()
        return carry

    lax.fori_loop(0, blocks, settle, 0)


def prior_kernel(
    count, end_ref, total_ref, prior_ref, totals, sent, swapped, pair, pairs, back, start, landed, near,
    near_sems, total_send, total_recv, swap_sems, pair_send, pair_recv, back_sems,
):
    heads = end_ref.shape[0]
    half = heads // 2
    greet((("seq", count),))
    me = lax.axis_index("seq")
    place = lax.rem(me, 2)
    partner = me + 1 - 2 * place
    group = me // 2
    groups = count // 2
    keep = place * half
    give = half - keep

    sent[...] = end_ref[pl.ds(give, half)].astype(BF16)
    swap = pltpu.make_async_remote_copy(
        src_ref=sent, dst_ref=swapped, send_sem=swap_sems.at[0], recv_sem=swap_sems.at[1],
        device_id={"seq": partner}, device_id_type=MESH,
    )
    swap.start()
    near_copy = pltpu.make_async_remote_copy(
        src_ref=total_ref, dst_ref=near, send_sem=near_sems.at[0], recv_sem=near_sems.at[1],
        device_id={"seq": partner}, device_id_type=MESH,
    )
    near_copy.start()
    total_copies = []
    for hop in range(1, count):
        copy = pltpu.make_async_remote_copy(
            src_ref=total_ref, dst_ref=totals.at[hop], send_sem=total_send.at[hop - 1],
            recv_sem=total_recv.at[hop - 1],
            device_id={"seq": lax.rem(me + hop, count)}, device_id_type=MESH,
        )
        copy.start()
        total_copies.append(copy)
    totals[0] = total_ref[...]
    near_copy.wait()
    swap.wait()

    def total_of(device):
        return totals[lax.rem(me - device + count, count)]

    odd = place.astype(F32)
    odd_fade = jnp.exp2(jnp.where(place == 0, near[...], total_ref[...]))
    even_fade = jnp.exp2(jnp.where(place == 0, total_ref[...], near[...]))
    for h in range(half):
        mine = end_ref[keep + h]
        other = swapped[h].astype(F32)
        first = odd * other + (1.0 - odd) * mine
        last = odd * mine + (1.0 - odd) * other
        row = jnp.where(place == 0, odd_fade[h : h + 1], odd_fade[half + h : half + h + 1])
        pair[h] = (row * first + last).astype(BF16)
        start[h] = first

    def pair_copy(hop):
        return pltpu.make_async_remote_copy(
            src_ref=pair, dst_ref=pairs.at[hop - 1], send_sem=pair_send.at[hop - 1],
            recv_sem=pair_recv.at[hop - 1],
            device_id={"seq": lax.rem(me + 2 * hop, count)}, device_id_type=MESH,
        )

    for hop in range(1, groups):

        @pl.when(group + hop < groups)
        def _():
            pair_copy(hop).start()

    for h in range(half):
        row = jnp.where(place == 0, even_fade[h : h + 1], even_fade[half + h : half + h + 1])
        back[h] = jnp.broadcast_to(row, back.shape[1:])

    for copy in total_copies:
        copy.wait()
    span = jnp.zeros(total_ref.shape, F32)
    prior_ref[pl.ds(keep, half)] = jnp.zeros((half,) + prior_ref.shape[1:], F32)
    for hop in range(1, groups):

        @pl.when(group >= hop)
        def _():
            pair_copy(hop).wait_recv()
            factor = jnp.exp2(span)
            for h in range(half):
                row = jnp.where(place == 0, factor[h : h + 1], factor[half + h : half + h + 1])
                prior_ref[keep + h] += row * pairs[hop - 1, h].astype(F32)

        source = lax.rem(group - hop + groups, groups) * 2
        span += total_of(source) + total_of(source + 1)

    for hop in range(1, groups):

        @pl.when(group + hop < groups)
        def _():
            pair_copy(hop).wait_send()

    for h in range(half):
        before = prior_ref[keep + h]
        later = back[h] * before + start[h]
        sent[h] = (odd * before + (1.0 - odd) * later).astype(BF16)
        prior_ref[keep + h] = odd * later + (1.0 - odd) * before
    answer = pltpu.make_async_remote_copy(
        src_ref=sent, dst_ref=landed, send_sem=back_sems.at[0], recv_sem=back_sems.at[1],
        device_id={"seq": partner}, device_id_type=MESH,
    )
    answer.start()
    answer.wait()
    prior_ref[pl.ds(give, half)] = landed[...].astype(F32)


def comm_params(number):
    return pltpu.CompilerParams(
        collective_id=number, has_side_effects=True, vmem_limit_bytes=VMEM_BYTES
    )


def carried_state(seq, end_state, totals, number):
    heads, size, width = end_state.shape
    half = heads // 2
    groups = seq // 2
    dma = pltpu.SemaphoreType.DMA
    whole = pl.BlockSpec(memory_space=pltpu.VMEM)
    return pl.pallas_call(
        functools.partial(prior_kernel, seq),
        out_shape=jax.ShapeDtypeStruct(end_state.shape, F32),
        in_specs=[whole, whole],
        out_specs=whole,
        scratch_shapes=[
            pltpu.VMEM((seq,) + totals.shape, F32),
            pltpu.VMEM((half, size, width), BF16),
            pltpu.VMEM((half, size, width), BF16),
            pltpu.VMEM((half, size, width), BF16),
            pltpu.VMEM((max(groups - 1, 1), half, size, width), BF16),
            pltpu.VMEM((half, size, width), F32),
            pltpu.VMEM((half, size, width), F32),
            pltpu.VMEM((half, size, width), BF16),
            pltpu.VMEM(totals.shape, F32),
            dma((2,)),
            dma((seq - 1,)),
            dma((seq - 1,)),
            dma((2,)),
            dma((max(groups - 1, 1),)),
            dma((max(groups - 1, 1),)),
            dma((2,)),
        ],
        compiler_params=comm_params(number),
        name=f"prior_{number}",
    )(end_state, totals)


def layer(
    seq, number, inputs, x_spec, gate, write_mat, read_mat, step_mat, decay_mat, skip, cols,
    out, out_spec, norm_of=None, send=None,
):
    heads = step_mat.shape[0]
    size = write_mat.shape[0]
    blocks = step_mat.shape[1] // BLOCK
    features = gate.shape[-1]
    width = features // heads
    wide = pl.BlockSpec((size, BLOCK), lambda b: (0, b))
    thin = pl.BlockSpec((heads, BLOCK), lambda b: (0, b))
    rows = pl.BlockSpec((1, BLOCK, features), lambda b: (b, 0, 0))
    params = pltpu.CompilerParams(vmem_limit_bytes=VMEM_BYTES)
    scale_of, extra, extra_specs = None, (), []
    shapes = [
        jax.ShapeDtypeStruct((heads, size, width), F32),
        jax.ShapeDtypeStruct((heads, LANES), F32),
    ]
    specs = [
        pl.BlockSpec((heads, size, width), lambda b: (0, 0, 0)),
        pl.BlockSpec((heads, LANES), lambda b: (0, 0)),
    ]
    if norm_of is not None:
        scale_of, extra, extra_specs = norm_of
        shapes.append(jax.ShapeDtypeStruct((blocks, BLOCK, features), BF16))
        specs.append(rows)
    made = pl.pallas_call(
        functools.partial(states_kernel, heads, scale_of),
        grid=(blocks,),
        out_shape=shapes,
        in_specs=[*extra_specs, x_spec, wide, thin, thin],
        out_specs=specs,
        compiler_params=params,
        name=f"states_{number}",
    )(*extra, inputs, write_mat, step_mat, decay_mat)
    prior = carried_state(seq, made[0], made[1], number)
    if norm_of is not None:
        inputs, x_spec = made[2], rows
    depth = -(-blocks // 8) * 8
    if send is not None:
        return send(skip, inputs, gate, write_mat, read_mat, step_mat, decay_mat, prior)
    return pl.pallas_call(
        functools.partial(main_kernel, heads, cols),
        grid=(blocks,),
        out_shape=(out, jax.ShapeDtypeStruct((depth, BLOCK), F32)),
        in_specs=[
            pl.BlockSpec(memory_space=pltpu.SMEM),
            x_spec,
            rows,
            wide,
            wide,
            thin,
            thin,
            pl.BlockSpec((heads, size, width), lambda b: (0, 0, 0)),
        ],
        out_specs=(out_spec, pl.BlockSpec((depth, BLOCK), lambda b: (0, 0))),
        scratch_shapes=[
            pltpu.VMEM((heads, size, width), F32), pltpu.VMEM((2, BLOCK, width), F32)
        ],
        compiler_params=params,
        name=f"main_{number}",
    )(skip, inputs, gate, write_mat, read_mat, step_mat, decay_mat, prior)


def body(
    seq, head, tokens_in, gate_rows, gate_cols, write_rows, read_rows, step_rows, decay_rows,
    skip_rows, norm_rows, write_cols, read_cols, step_cols, decay_cols, skip_cols, norm_cols,
):
    grid_rows, grid_cols, features = tokens_in.shape
    blocks = grid_rows * grid_cols // BLOCK
    high = BLOCK // grid_cols
    local_cols = grid_cols // seq
    all_rows = grid_rows * seq
    per_col = all_rows // BLOCK
    slabs = BLOCK // grid_rows
    inner = features * head
    dma = pltpu.SemaphoreType.DMA
    anywhere = pl.BlockSpec(memory_space=pl.ANY)
    whole = pl.BlockSpec(memory_space=pltpu.VMEM)
    rows = pl.BlockSpec((1, BLOCK, features), lambda b: (b, 0, 0))

    heads, size = step_rows.shape[0], write_rows.shape[0]
    width = features // heads
    depth = -(-blocks // 8) * 8
    send = pl.pallas_call(
        functools.partial(trade_kernel, seq, head, inner, heads, grid_cols),
        out_shape=(
            jax.ShapeDtypeStruct((seq, local_cols, grid_rows, features), BF16),
            jax.ShapeDtypeStruct((seq * depth, BLOCK), F32),
        ),
        in_specs=[pl.BlockSpec(memory_space=pltpu.SMEM), anywhere, anywhere] + [whole] * 5,
        out_specs=(anywhere, whole),
        scratch_shapes=[
            pltpu.VMEM((blocks, BLOCK, features), BF16),
            pltpu.VMEM((blocks, BLOCK, features), BF16),
            pltpu.VMEM((blocks, seq, local_cols, high, features), BF16),
            pltpu.VMEM((depth, BLOCK), F32),
            pltpu.VMEM((heads, size, width), F32),
            pltpu.VMEM((2, BLOCK, width), F32),
            pltpu.VMEM((head - 1, depth, BLOCK), F32),
            pltpu.VMEM((depth, BLOCK), F32),
            dma((2, blocks)),
            dma((head - 1,)), dma((head - 1,)),
            dma((seq - 1,)), dma((seq - 1,)),
            dma((seq - 1, blocks)), dma((seq - 1, blocks)), dma((blocks,)),
        ],
        compiler_params=comm_params(2),
        name="trade",
    )
    hidden, scales = layer(
        seq, 0, tokens_in.reshape(blocks, BLOCK, features), rows,
        gate_rows.reshape(blocks, BLOCK, features),
        write_rows, read_rows, step_rows, decay_rows, skip_rows, grid_cols, None, None, None, send,
    )
    gate = jnp.transpose(gate_cols, (1, 0, 2)).reshape(local_cols * per_col, BLOCK, features)
    gated, squares = layer(
        seq, 1, hidden,
        pl.BlockSpec(
            (slabs, 1, grid_rows, features), lambda b: (b % per_col, b // per_col, 0, 0)
        ),
        gate, write_cols, read_cols, step_cols, decay_cols, skip_cols, 1,
        jax.ShapeDtypeStruct((local_cols * per_col, BLOCK, features), F32), rows,
        (
            functools.partial(column_scale, local_cols, per_col, grid_rows, grid_cols),
            (lax.axis_index("seq").reshape(1), scales, norm_rows.reshape(1, features)),
            [
                pl.BlockSpec(memory_space=pltpu.SMEM),
                pl.BlockSpec((slabs * depth, BLOCK), lambda b: (b % per_col, 0)),
                pl.BlockSpec((1, features), lambda b: (0, 0)),
            ],
        ),
    )
    squares = pl.pallas_call(
        functools.partial(sum_kernel, head),
        out_shape=jax.ShapeDtypeStruct(squares.shape, F32),
        in_specs=[whole],
        out_specs=whole,
        scratch_shapes=[
            pltpu.VMEM((head - 1,) + squares.shape, F32), dma((head - 1,)), dma((head - 1,)),
        ],
        compiler_params=comm_params(3),
        name="squares",
    )(squares)
    part = BLOCK // local_cols
    out_shape, out_spec = (all_rows, local_cols, features), (part, local_cols, features)
    if local_cols == 1:
        out_shape, out_spec = (all_rows, features), (part, features)
    result = pl.pallas_call(
        functools.partial(norm_kernel, inner, per_col),
        grid=(all_rows // part,),
        out_shape=jax.ShapeDtypeStruct(out_shape, BF16),
        in_specs=[
            pl.BlockSpec((local_cols, part, features), lambda q: (0, q, 0)),
            pl.BlockSpec(squares.shape, lambda q: (0, 0)),
            pl.BlockSpec((1, features), lambda q: (0, 0)),
        ],
        out_specs=pl.BlockSpec(out_spec, lambda q: (q,) + (0,) * (len(out_spec) - 1)),
        scratch_shapes=[pltpu.VMEM((2, BLOCK, LANES), F32)],
        compiler_params=pltpu.CompilerParams(vmem_limit_bytes=VMEM_BYTES),
        name="norm",
    )(gated.reshape(local_cols, all_rows, features), squares, norm_cols.reshape(1, features))
    return result.reshape(all_rows, local_cols, features)


def solution(mesh):
    placed = (
        P("seq", None, "head"),
        P("seq", None, "head"),
        P(None, "seq", "head"),
        P(None, "seq"),
        P(None, "seq"),
        P("head", "seq"),
        P("head", "seq"),
        P("head"),
        P("head"),
        P(None, "seq"),
        P(None, "seq"),
        P("head", "seq"),
        P("head", "seq"),
        P("head"),
        P("head"),
    )
    return jax.shard_map(
        functools.partial(body, mesh.shape["seq"], mesh.shape["head"]),
        mesh=mesh, in_specs=placed, out_specs=P(None, "seq", "head"), check_vma=False,
    )
```

profile of v0, /device:TPU:25, one launch (start us, length us, event | category | flops | bytes accessed | tf_op | source)
XLA Modules:
  0.0 158.1 jit_solution(17989692695086367431)
XLA Ops:
  0.0 5.1 %states_0.1 = (f32[12,64,128]{2,1,0:T(8,128)}, f32[12,128]{1,0:T(8,128)}) custom-call(bf16[4,256,1536]{2,1,0:T(8,128)(2,1)} %bitcast.7, bf16[64,1024]{1,0:T(8,128)(2,1)} %write_ref.2, f32[12,1024]{1,0:T(8,128)} %step_ref.2, f32[12,1024]{1,0:T(8,128)} %decay_ref.2), custom_call_target="tpu_custom_call" | custom-call | tf_op jit(solution)/shard_map/states_0/pallas_call | solution.py:496
  5.1 18.4 %prior_0.1.prior_ref = f32[12,64,128]{2,1,0:T(8,128)} custom-call(f32[12,64,128]{2,1,0:T(8,128)} %get-tuple-element.14.end_ref, f32[12,128]{1,0:T(8,128)} %get-tuple-element.15.total_ref), custom_call_target="tpu_custom_call" | custom-call | tf_op jit(solution)/shard_map/prior_0/pallas_call | solution.py:442
  23.5 0.0 copy-start.1
  23.6 77.2 %trade.1 = (bf16[8,4,32,1536]{3,2,1,0:T(8,128)(2,1)}, f32[64,256]{1,0:T(8,128)}) custom-call(f32[12]{0:T(128)} %skip_ref.2, bf16[4,256,1536]{2,1,0:T(8,128)(2,1)} %bitcast.8, bf16[4,256,1536]{2,1,0:T(8,128)(2,1)} %bitcast.9, bf16[64,1024]{1,0:T(8,128)(2,1)} %write_ref.2, bf16[64,1024]{1,0:T(8,128)(2,1)} %read_ref.2, f32[12,1024]{1,0:T(8,128)} %step_ref.2, ...), custom_call_target="tpu_custom_call" | custom-call | tf_op jit(solution)/shard_map/trade/pallas_call | solution.py:510
  100.8 0.0 copy-start
  100.8 0.0 copy-done.1
  100.8 0.6 reshape.18.refs_2_
  101.4 6.8 %states_1.1 = (f32[12,64,128]{2,1,0:T(8,128)}, f32[12,128]{1,0:T(8,128)}, bf16[4,256,1536]{2,1,0:T(8,128)(2,1)}) custom-call(s32[1]{0:T(128)} %bitcast.refs_0_, f32[64,256]{1,0:T(8,128)} %get-tuple-element.16.refs_1_, f32[1,1536]{1,0:T(1,128)} %reshape.18.refs_2_, bf16[8,4,32,1536]{3,2,1,0:T(8,128)(2,1)} %get-tuple-element.17.refs_3_, ...), custom_call_target="tpu_custom_call" | custom-call | tf_op jit(solution)/shard_map/states_1/pallas_call | solution.py:496
  108.3 18.1 %prior_1.1.prior_ref = f32[12,64,128]{2,1,0:T(8,128)} custom-call(f32[12,64,128]{2,1,0:T(8,128)} %get-tuple-element.19.end_ref, f32[12,128]{1,0:T(8,128)} %get-tuple-element.20.total_ref), custom_call_target="tpu_custom_call" | custom-call | tf_op jit(solution)/shard_map/prior_1/pallas_call | solution.py:442
  126.3 0.0 copy-done
  126.3 2.3 %copy.18 = bf16[256,4,1536]{2,0,1:T(8,128)(2,1)} copy(bf16[256,4,1536]{2,1,0:T(4,128)(2,1)S(1)} %copy-done) | data formatting | bytes 6291456 | tf_op args[2]
  128.6 0.0 copy-start.2
  128.6 13.1 %main_1.1 = (f32[4,256,1536]{2,1,0:T(8,128)}, f32[8,256]{1,0:T(8,128)}) custom-call(f32[12]{0:T(128)} %skip_ref.3, bf16[4,256,1536]{2,1,0:T(8,128)(2,1)} %get-tuple-element.18.x_ref, bf16[4,256,1536]{2,1,0:T(8,128)(2,1)} %bitcast.6, bf16[64,1024]{1,0:T(8,128)(2,1)} %write_ref.3, bf16[64,1024]{1,0:T(8,128)(2,1)} %read_ref.3, f32[12,1024]{1,0:T(8,128)} %step_ref.3, ...), custom_call_target="tpu_custom_call" | custom-call | tf_op jit(solution)/shard_map/main_1/pallas_call | solution.py:511
  141.7 9.1 %squares.1.squares_ref = f32[8,256]{1,0:T(8,128)} custom-call(f32[8,256]{1,0:T(8,128)} %get-tuple-element.22.own_ref), custom_call_target="tpu_custom_call" | custom-call | tf_op jit(solution)/shard_map/squares/pallas_call | solution.py:602
  150.8 0.0 copy-done.2
  150.8 0.6 reshape.19.gain_ref
  151.4 6.7 %norm.1 = bf16[256,4,1536]{2,1,0:T(4,128)(2,1)} custom-call(f32[4,256,1536]{2,1,0:T(8,128)} %get-tuple-element.21.gated_ref, f32[8,256]{1,0:T(8,128)} %squares.1.squares_ref, f32[1,1536]{1,0:T(1,128)} %reshape.19.gain_ref), custom_call_target="tpu_custom_call" | custom-call | tf_op jit(solution)/shard_map/norm/pallas_call | solution.py:617
Async XLA Ops:
  23.5 77.3 %copy-start.1 = (f32[1536]{0:T(1024)S(1)}, f32[1536]{0:T(1024)}, u32[]{:S(2)}) copy-start(f32[1536]{0:T(1024)} %param.23) | copy-start | bytes 18436
  100.8 25.5 %copy-start = (bf16[256,4,1536]{2,1,0:T(4,128)(2,1)S(1)}, bf16[256,4,1536]{2,1,0:T(4,128)(2,1)}, u32[]{:S(2)}) copy-start(bf16[256,4,1536]{2,1,0:T(4,128)(2,1)} %param.17) | copy-start | bytes 9437188
  128.6 22.2 %copy-start.2 = (f32[1536]{0:T(1024)S(1)}, f32[1536]{0:T(1024)}, u32[]{:S(2)}) copy-start(f32[1536]{0:T(1024)} %param.29) | copy-start | bytes 18436
where the time goes:
time: 158 us
  Pallas kernels  155 us (98%)
  local copies, waits for them, and re-layouts  3.48 us (2%)
    pallas_call x1, Pallas kernels, layer(): send(skip, inputs, gate, write_mat, read_mat, step_mat, decay_mat, prior)  77.2 us
    pallas_call x2, Pallas kernels, carried_state(): pl.pallas_call(functools.partial(prior_kernel, seq), out_shape=jax.ShapeD...  36.5 us
    pallas_call x1, Pallas kernels, layer(): pl.pallas_call(functools.partial(main_kernel, heads, cols), grid=(blocks,...  13.1 us
    pallas_call x2, Pallas kernels, layer(): pl.pallas_call(functools.partial(states_kernel, heads, scale_of), grid=(b...  12 us
    pallas_call x1, Pallas kernels, body(): pl.pallas_call(functools.partial(sum_kernel, head), out_shape=jax.ShapeDt...  9.11 us
    pallas_call x1, Pallas kernels, body(): pl.pallas_call(functools.partial(norm_kernel, inner, per_col), grid=(all_...  6.68 us

commit v1 on v0

v1 whole, which is shorter than its diff:
```python
import functools
import jax
import jax.numpy as jnp
from jax import lax
from jax.experimental import pallas as pl
from jax.experimental.pallas import tpu as pltpu
from jax.sharding import PartitionSpec as P

BLOCK = 256
HALF = 128
LANES = 128
CHUNK = 2
EPSILON = 1e-05
LOG2E = 1.4426950408889634
HIGHEST = lax.Precision.HIGHEST
MESH = pl.DeviceIdType.MESH
F32 = jnp.float32
BF16 = jnp.bfloat16
VMEM_BYTES = 60 * 1024 * 1024


def contract(a, b, dims, precision=None):
    return lax.dot_general(
        a, b, (dims, ((), ())), precision=precision, preferred_element_type=F32
    )


def iota(shape, axis):
    return lax.broadcasted_iota(jnp.int32, shape, axis)


def round_up(value, step):
    return -(-value // step) * step


def split(value, count):
    parts = []
    for _ in range(count - 1):
        part = value.astype(BF16)
        parts.append(part)
        value = value - part.astype(F32)
    parts.append(value.astype(BF16))
    return parts


def span_of(b):
    return pl.ds(pl.multiple_of(b * BLOCK, BLOCK), BLOCK)


class Layer:
    def __init__(self, **refs):
        self.__dict__.update(refs)


def prepare_sums(layer):
    heads, length = layer.decay.shape
    blocks = length // BLOCK
    padded = layer.cum.shape[1]
    layer.stage[...] = jnp.zeros_like(layer.stage)
    for p, part in enumerate(split(layer.decay[...] * LOG2E, 3)):
        for b in range(blocks):
            layer.stage[b, p, :heads] = part[:, b * BLOCK : (b + 1) * BLOCK]
    upper = (iota((BLOCK, BLOCK), 0) <= iota((BLOCK, BLOCK), 1)).astype(BF16)
    sums = contract(layer.stage[...].reshape(blocks * 3 * padded, BLOCK), upper, ((1,), (0,)))
    sums = sums.reshape(blocks, 3, padded, BLOCK)
    run = jnp.zeros((padded, 1), F32)
    for b in range(blocks):
        cum = sums[b, 0] + sums[b, 1] + sums[b, 2]
        final = cum[:, BLOCK - 1 :]
        layer.cum[b] = cum
        layer.weights[b, :heads] = (
            jnp.exp2(final[:heads] - cum[:heads]) * layer.step[:, b * BLOCK : (b + 1) * BLOCK]
        )
        layer.fades[b] = jnp.broadcast_to(jnp.exp2(final), (padded, LANES))
        layer.before[b] = jnp.broadcast_to(jnp.exp2(run), (padded, LANES))
        run = run + final
    layer.total[...] = jnp.broadcast_to(run, (padded, LANES))


def prepare_scores(layer):
    blocks = layer.cum.shape[0]
    lower = (iota((BLOCK, BLOCK), 0) >= iota((BLOCK, BLOCK), 1)).astype(F32)

    def block(b, carry):
        across = jnp.transpose(layer.cum[b])
        layer.across[b] = across
        layer.lifting[b] = jnp.exp2(across)
        read = layer.read[:, span_of(b)]
        layer.scores[b] = contract(read, layer.write[:, span_of(b)], ((0,), (0,))) * lower
        read32 = read.astype(F32)
        layer.read_t[b] = jnp.transpose(jnp.concatenate([read32, read32], axis=0)).astype(BF16)
        return carry

    lax.fori_loop(0, blocks, block, 0)


def lanes_of(h):
    return slice(h * LANES, (h + 1) * LANES)


def add_state(layer, b, h, write32, own):
    loaded = (write32 * layer.weights[b, h : h + 1, :]).astype(BF16)
    gained = contract(loaded, own, ((1,), (0,)))
    held = layer.state[h]
    layer.local[b, h] = held
    layer.state[h] = layer.fades[b, h : h + 1, :] * held + gained


def inner_block(layer, b, h, own):
    across = layer.across[b, :, h : h + 1]
    cum = layer.cum[b, h : h + 1, :]
    step = layer.step[h : h + 1, span_of(b)]
    top, low = slice(0, HALF), slice(HALF, BLOCK)

    def mix(rows, cols, diagonal):
        spread = across[rows] - cum[:, cols]
        if diagonal:
            spread = jnp.minimum(spread, 0.0)
        return (jnp.exp2(spread) * layer.scores[b, rows, cols] * step[:, cols]).astype(BF16)

    skip = layer.skip[h]
    first = contract(mix(top, top, True), own[top], ((1,), (0,)))
    layer.inner[b, top, lanes_of(h)] = first + skip * own[top].astype(F32)
    both = jnp.concatenate([mix(low, top, False), mix(low, low, True)], axis=1)
    second = contract(both, own, ((1,), (0,)))
    layer.inner[b, low, lanes_of(h)] = second + skip * own[low].astype(F32)


def finish_block(layer, b, hs, store):
    held = jnp.concatenate(
        [layer.before[b, h : h + 1, :] * layer.prior[h] + layer.local[b, h] for h in hs], axis=1
    )
    parts = jnp.concatenate(split(held, 2), axis=0)
    from_state = contract(layer.read_t[b], parts, ((1,), (0,)))
    squares = jnp.zeros((BLOCK, LANES), F32)
    for i, h in enumerate(hs):
        out = layer.inner[b, :, lanes_of(h)]
        out += layer.lifting[b, :, h : h + 1] * from_state[:, i * LANES : (i + 1) * LANES]
        gate = layer.gate[b, :, lanes_of(h)].astype(F32)
        gated = out * (gate / (1.0 + jnp.exp2(gate * -LOG2E)))
        squares += gated * gated
        store(b, h, gated)
    layer.squares[b] += squares


def reduce_squares(layer, rows_ref):
    blocks = layer.squares.shape[0]
    rows_ref[...] = jnp.zeros_like(rows_ref)
    for b in range(blocks):
        parts = jnp.concatenate(split(layer.squares[b], 2), axis=1)
        row = contract(jnp.ones((8, 2 * LANES), BF16), parts, ((1,), (1,)))
        rows_ref[b : b + 1, :] = row[:1]


def column_scale(column, grid_rows, grid_cols, scales):
    high = BLOCK // grid_cols
    shape = (BLOCK, scales.shape[0])
    row = iota(shape, 0)
    depth = scales.shape[0] * grid_rows // BLOCK
    source = (row // grid_rows) * depth + (row % grid_rows) // high
    picked = contract((iota(shape, 1) == source).astype(F32), scales, ((1,), (0,)), HIGHEST)
    lane = (iota((BLOCK, BLOCK), 0) % high) * grid_cols + column
    return jnp.sum(jnp.where(iota((BLOCK, BLOCK), 1) == lane, picked, 0.0), axis=1, keepdims=True)


def greet_signal(axes):
    barrier = pltpu.get_barrier_semaphore()
    for axis, count in axes:
        me = lax.axis_index(axis)
        for hop in range(1, count):
            pl.semaphore_signal(
                barrier, inc=1, device_id={axis: lax.rem(me + hop, count)}, device_id_type=MESH
            )


def greet_wait(axes):
    pl.semaphore_wait(
        pltpu.get_barrier_semaphore(), sum(count - 1 for _, count in axes)
    )


def head_sum(count, own_ref, held, send_sems, recv_sems):
    me = lax.axis_index("head")
    copies = []
    for hop in range(1, count):
        copy = pltpu.make_async_remote_copy(
            src_ref=own_ref,
            dst_ref=held.at[hop - 1],
            send_sem=send_sems.at[hop - 1],
            recv_sem=recv_sems.at[hop - 1],
            device_id={"head": lax.rem(me + hop, count)},
            device_id_type=MESH,
        )
        copy.start()
        copies.append(copy)
    for copy in copies:
        copy.wait()
    total = own_ref[...]
    for hop in range(1, count):
        total += held[hop - 1]
    return total


class Exchange:
    def __init__(self, seq, layer, sent, swapped, passed, came, near, swap_sems, near_sems, pass_sems):
        self.layer, self.sent, self.swapped = layer, sent, swapped
        self.passed, self.came, self.near = passed, came, near
        self.swap_sems, self.near_sems, self.pass_sems = swap_sems, near_sems, pass_sems
        me = lax.axis_index("seq")
        self.place = lax.rem(me, 2)
        self.partner = me + 1 - 2 * self.place
        self.group = me // 2
        self.groups = seq // 2
        self.ahead = lax.rem(me + 2, seq)

    def near_copy(self):
        return pltpu.make_async_remote_copy(
            src_ref=self.layer.total, dst_ref=self.near, send_sem=self.near_sems.at[0],
            recv_sem=self.near_sems.at[1], device_id={"seq": self.partner}, device_id_type=MESH,
        )

    def swap_copy(self, c, part):
        return pltpu.make_async_remote_copy(
            src_ref=self.sent.at[part], dst_ref=self.swapped.at[part],
            send_sem=self.swap_sems.at[0, c], recv_sem=self.swap_sems.at[1, c],
            device_id={"seq": self.partner}, device_id_type=MESH,
        )

    def pass_copy(self, c, part):
        return pltpu.make_async_remote_copy(
            src_ref=self.passed.at[part], dst_ref=self.came.at[part],
            send_sem=self.pass_sems.at[0, c], recv_sem=self.pass_sems.at[1, c],
            device_id={"seq": self.ahead}, device_id_type=MESH,
        )

    def swap(self, c, part):
        for h in range(part.start, part.start + part.size):
            self.sent[h] = self.layer.state[h].astype(BF16)
        self.swap_copy(c, part).start()

    def fades(self):
        self.near_copy().wait()
        mine, other = self.layer.total[...], self.near[...]
        even = self.place == 0
        return jnp.exp2(jnp.where(even, mine, other)), jnp.exp2(jnp.where(even, other, mine))

    def step(self, c, part, fades):
        layer = self.layer
        first_fade, last_fade = fades
        even = self.place == 0
        self.swap_copy(c, part).wait()

        @pl.when(self.group > 0)
        def _():
            self.pass_copy(c, part).wait_recv()

        for h in range(part.start, part.start + part.size):
            mine, other = layer.state[h], self.swapped[h].astype(F32)
            first, last = jnp.where(even, mine, other), jnp.where(even, other, mine)
            before = self.came[h].astype(F32)
            middle = first_fade[h : h + 1] * before + first
            self.passed[h] = (last_fade[h : h + 1] * middle + last).astype(BF16)
            layer.prior[h] = jnp.where(even, before, middle)

        @pl.when(self.group < self.groups - 1)
        def _():
            self.pass_copy(c, part).start()

    def settle(self, parts):
        for c, part in enumerate(parts):

            @pl.when(self.group < self.groups - 1)
            def _(c=c, part=part):
                self.pass_copy(c, part).wait_send()


def fused_kernel(
    seq, head_count, inner, grid_cols, local_cols, per_col,
    skip1, skip2, x_hbm, gate1_hbm, gate2_hbm, write1, read1, step1, decay1, gain1,
    write2, read2, step2, decay2,
    out_hbm, total_ref,
    x, gate1, gate2, sendbuf, recvbuf, hidden, outbuf, innerbuf, turned,
    stage, cum1, cum2, weights, fades1, fades2, before1, before2, total1, total2, across, lifting,
    scores, read_t, state, local, prior, squares, rows1, held1, held2, scale, scales, column,
    sent1, swapped1, passed1, came1, near1, sent2, swapped2, passed2, came2, near2,
    load_sems, bulk_send, bulk_recv, keep_sems, sum1, sum2, scale_send, scale_recv, out_sems,
    swap1_sems, near1_sems, pass1_sems, swap2_sems, near2_sems, pass2_sems,
):
    axes = (("seq", seq), ("head", head_count))
    me = lax.axis_index("seq")
    blocks, _, features = x.shape
    heads = features // LANES
    high = BLOCK // grid_cols
    grid_rows = blocks * high
    slabs = BLOCK // grid_rows
    parts = [pl.ds(c, min(CHUNK, heads - c)) for c in range(0, heads, CHUNK)]
    numbers = [range(part.start, part.start + part.size) for part in parts]
    chunks = len(parts)
    greet_signal(axes)

    def load(b):
        return pltpu.make_async_copy(x_hbm.at[b], x.at[b], load_sems.at[0, b])

    gate_loads = [
        pltpu.make_async_copy(gate1_hbm, gate1, load_sems.at[1, 0]),
        pltpu.make_async_copy(gate2_hbm, gate2, load_sems.at[2, 0]),
    ]
    for b in range(blocks):
        load(b).start()
    for copy in gate_loads:
        copy.start()

    shared = dict(
        stage=stage, weights=weights, across=across, lifting=lifting, scores=scores,
        read_t=read_t, state=state, local=local, prior=prior, squares=squares, inner=innerbuf,
    )
    one = Layer(
        skip=skip1, gate=gate1, write=write1, read=read1, step=step1, decay=decay1, cum=cum1,
        fades=fades1, before=before1, total=total1, **shared,
    )
    two = Layer(
        skip=skip2, gate=gate2, write=write2, read=read2, step=step2, decay=decay2, cum=cum2,
        fades=fades2, before=before2, total=total2, **shared,
    )
    ex1 = Exchange(
        seq, one, sent1, swapped1, passed1, came1, near1, swap1_sems, near1_sems, pass1_sems
    )
    ex2 = Exchange(
        seq, two, sent2, swapped2, passed2, came2, near2, swap2_sems, near2_sems, pass2_sems
    )

    @pl.when(ex1.group == 0)
    def _():
        came1[...] = jnp.zeros_like(came1)
        came2[...] = jnp.zeros_like(came2)

    prepare_sums(one)
    state[...] = jnp.zeros_like(state)

    def states1(b, carry):
        load(b).wait()
        write32 = write1[:, span_of(b)].astype(F32)
        for h in range(heads):
            add_state(one, b, h, write32, x[b, :, lanes_of(h)])
        return carry

    lax.fori_loop(0, blocks, states1, 0)
    greet_wait(axes)
    ex1.near_copy().start()
    for c, part in enumerate(parts):
        ex1.swap(c, part)

    prepare_scores(one)
    squares[...] = jnp.zeros_like(squares)

    def inner1(c):
        def block(b, carry):
            for h in numbers[c]:
                inner_block(one, b, h, x[b, :, lanes_of(h)])
            return carry

        lax.fori_loop(0, blocks, block, 0)

    def store1(b, h, gated):
        slot = turned.at[h % 2]
        slot[...] = gated
        for col in range(grid_cols):
            sendbuf[col // local_cols, col % local_cols, b, :, lanes_of(h)] = slot[
                pl.ds(col, high, stride=grid_cols), :
            ].astype(BF16)

    def finish1(c):
        def block(b, carry):
            finish_block(one, b, numbers[c], store1)
            return carry

        lax.fori_loop(0, blocks, block, 0)

    def wide(c):
        return pl.ds(parts[c].start * LANES, parts[c].size * LANES)

    def bulk(c, hop):
        to = lax.rem(me - hop + seq, seq)
        return pltpu.make_async_remote_copy(
            src_ref=sendbuf.at[to, :, :, :, wide(c)],
            dst_ref=recvbuf.at[me, :, :, :, wide(c)],
            send_sem=bulk_send.at[hop - 1, c],
            recv_sem=bulk_recv.at[hop - 1, c],
            device_id={"seq": to},
            device_id_type=MESH,
        )

    def keep(c):
        return pltpu.make_async_copy(
            sendbuf.at[me, :, :, :, wide(c)], recvbuf.at[me, :, :, :, wide(c)], keep_sems.at[c]
        )

    def send_all(c):
        for hop in range(1, seq):
            bulk(c, hop).start()
        keep(c).start()

    inner1(0)
    fades = ex1.fades()
    for copy in gate_loads:
        copy.wait()
    ex1.step(0, parts[0], fades)
    finish1(0)
    for hop in range(1, seq):

        @pl.when(hop <= me)
        def _(hop=hop):
            bulk(0, hop).start()

    for c in range(1, chunks):
        ex1.step(c, parts[c], fades)
    for hop in range(1, seq):

        @pl.when(hop > me)
        def _(hop=hop):
            bulk(0, hop).start()

    keep(0).start()
    for c in range(1, chunks):
        inner1(c)
        finish1(c)
        if c == 1:
            send_all(c)
    reduce_squares(one, rows1)
    scale[...] = lax.rsqrt(head_sum(head_count, rows1, held1, sum1.at[0], sum1.at[1]) / inner + EPSILON)
    depth = scale.shape[0]
    mine = pl.ds(pl.multiple_of(me * depth, depth), depth)
    scale_copies = []
    for hop in range(1, seq):
        copy = pltpu.make_async_remote_copy(
            src_ref=scale,
            dst_ref=scales.at[mine],
            send_sem=scale_send.at[hop - 1],
            recv_sem=scale_recv.at[hop - 1],
            device_id={"seq": lax.rem(me - hop + seq, seq)},
            device_id_type=MESH,
        )
        copy.start()
        scale_copies.append(copy)
    for c in range(2, chunks):
        send_all(c)
    scales[mine, :] = scale[...]

    prepare_sums(two)
    prepare_scores(two)
    state[...] = jnp.zeros_like(state)
    squares[...] = jnp.zeros_like(squares)
    ex2.near_copy().start()
    for copy in scale_copies:
        copy.wait()

    def columns(b, carry):
        window = pl.ds(
            pl.multiple_of(lax.rem(b, per_col) * slabs * depth, slabs * depth), slabs * depth
        )
        picked = column_scale(me * local_cols + b // per_col, grid_rows, grid_cols, scales[window, :])
        column[b] = jnp.broadcast_to(picked, (BLOCK, LANES))
        return carry

    lax.fori_loop(0, blocks, columns, 0)

    def arrive(c):
        keep(c).wait()
        for hop in range(1, seq):
            bulk(c, hop).wait()

    def states2(c):
        def block(b, carry):
            write32 = write2[:, span_of(b)].astype(F32)
            slab = pl.ds(lax.rem(b, per_col) * slabs, slabs)
            for h in numbers[c]:
                lanes = lanes_of(h)
                own = recvbuf[slab, b // per_col, :, :, lanes].astype(F32).reshape(BLOCK, LANES)
                own = (own * column[b] * gain1[:, lanes]).astype(BF16)
                hidden[b, :, lanes] = own
                add_state(two, b, h, write32, own)
            return carry

        lax.fori_loop(0, blocks, block, 0)

    def inner2(c):
        def block(b, carry):
            for h in numbers[c]:
                inner_block(two, b, h, hidden[b, :, lanes_of(h)])
            return carry

        lax.fori_loop(0, blocks, block, 0)

    def store2(b, h, gated):
        outbuf[b, :, lanes_of(h)] = gated.astype(BF16)

    def put(c):
        return pltpu.make_async_copy(
            outbuf.at[:, :, wide(c)], out_hbm.at[:, :, wide(c)], out_sems.at[c]
        )

    def finish2(c):
        def block(b, carry):
            finish_block(two, b, numbers[c], store2)
            return carry

        lax.fori_loop(0, blocks, block, 0)
        put(c).start()

    last = chunks - 1
    early = max(last - 1, 0)
    fades = None
    for c in range(chunks):
        if c == last and last > 0:
            fades = ex2.fades()
            for e in range(early):
                ex2.step(e, parts[e], fades)
            for e in range(early):
                finish2(e)
        arrive(c)
        states2(c)
        ex2.swap(c, parts[c])
        if c < last:
            inner2(c)
    if fades is None:
        fades = ex2.fades()
    for c in range(early, last):
        ex2.step(c, parts[c], fades)
    inner2(last)
    ex2.step(last, parts[last], fades)
    for c in range(early, chunks):
        finish2(c)
    reduce_squares(two, rows1)
    total_ref[...] = head_sum(head_count, rows1, held2, sum2.at[0], sum2.at[1])
    for c in range(chunks):
        put(c).wait()
    ex1.settle(parts)
    ex2.settle(parts)


def norm_kernel(inner, per_col, gated_ref, squares_ref, gain_ref, out_ref, turned):
    cols, rows, features = gated_ref.shape
    square = (BLOCK, BLOCK)
    start = pl.program_id(0) * rows
    lane = start % BLOCK + iota(square, 0) % rows
    sums = contract((lane == iota(square, 1)).astype(F32), squares_ref[...], ((1,), (1,)), HIGHEST)
    block = (iota(sums.shape, 0) // rows) * per_col + start // BLOCK
    sums = jnp.sum(jnp.where(iota(sums.shape, 1) == block, sums, 0.0), axis=1, keepdims=True)
    scaled = lax.rsqrt(sums / inner + EPSILON)
    for at in range(0, features, LANES):
        lanes = slice(at, at + LANES)
        gated = gated_ref[:, :, lanes].astype(F32).reshape(BLOCK, LANES)
        result = gated * scaled * gain_ref[:, lanes]
        if cols > 1:
            slot = turned.at[at // LANES % 2]
            for c in range(cols):
                slot[pl.ds(c, rows, stride=cols), :] = result[c * rows : (c + 1) * rows]
            out_ref[:, :, lanes] = slot[...].reshape(rows, cols, LANES).astype(BF16)
        else:
            out_ref[:, lanes] = result.astype(BF16)


def body(
    seq, head, tokens_in, gate_rows, gate_cols, write_rows, read_rows, step_rows, decay_rows,
    skip_rows, norm_rows, write_cols, read_cols, step_cols, decay_cols, skip_cols, norm_cols,
):
    grid_rows, grid_cols, features = tokens_in.shape
    blocks = grid_rows * grid_cols // BLOCK
    high = BLOCK // grid_cols
    local_cols = grid_cols // seq
    all_rows = grid_rows * seq
    per_col = all_rows // BLOCK
    inner = features * head
    heads, size = step_rows.shape[0], write_rows.shape[0]
    width = features // heads
    depth = round_up(blocks, 8)
    padded = round_up(heads, 16)
    chunks = -(-heads // CHUNK)
    dma = pltpu.SemaphoreType.DMA
    anywhere = pl.BlockSpec(memory_space=pl.ANY)
    whole = pl.BlockSpec(memory_space=pltpu.VMEM)
    smem = pl.BlockSpec(memory_space=pltpu.SMEM)
    vmem = pltpu.VMEM
    tokens = (blocks, BLOCK, features)
    packed = (seq, local_cols, blocks, high, features)
    sums = (blocks, padded, BLOCK)
    rows = (blocks, padded, LANES)
    total = (padded, LANES)
    tall = (blocks, BLOCK, padded)
    states = (heads, size, width)
    exchange = [vmem(states, BF16)] * 4 + [vmem(total, F32)]
    gate = jnp.transpose(gate_cols, (1, 0, 2)).reshape(tokens)
    gated, squares = pl.pallas_call(
        functools.partial(fused_kernel, seq, head, inner, grid_cols, local_cols, per_col),
        out_shape=(
            jax.ShapeDtypeStruct(tokens, BF16),
            jax.ShapeDtypeStruct((depth, BLOCK), F32),
        ),
        in_specs=[smem, smem] + [anywhere] * 3 + [whole] * 9,
        out_specs=(anywhere, whole),
        scratch_shapes=[
            vmem(tokens, BF16), vmem(tokens, BF16), vmem(tokens, BF16),
            vmem(packed, BF16), vmem(packed, BF16), vmem(tokens, BF16), vmem(tokens, BF16),
            vmem(tokens, F32), vmem((2, BLOCK, LANES), F32),
            vmem((blocks, 3, padded, BLOCK), BF16), vmem(sums, F32), vmem(sums, F32),
            vmem(sums, F32), vmem(rows, F32), vmem(rows, F32), vmem(rows, F32), vmem(rows, F32),
            vmem(total, F32), vmem(total, F32), vmem(tall, F32), vmem(tall, F32),
            vmem((blocks, BLOCK, BLOCK), F32), vmem((blocks, BLOCK, 2 * size), BF16),
            vmem(states, F32), vmem((blocks,) + states, F32), vmem(states, F32),
            vmem((blocks, BLOCK, LANES), F32), vmem((depth, BLOCK), F32),
            vmem((head - 1, depth, BLOCK), F32), vmem((head - 1, depth, BLOCK), F32),
            vmem((depth, BLOCK), F32), vmem((seq * depth, BLOCK), F32),
            vmem((blocks, BLOCK, LANES), F32),
            *exchange, *exchange,
            dma((3, blocks)), dma((seq - 1, chunks)), dma((seq - 1, chunks)), dma((chunks,)),
            dma((2, head - 1)), dma((2, head - 1)), dma((seq - 1,)), dma((seq - 1,)),
            dma((chunks,)),
            dma((2, chunks)), dma((2,)), dma((2, chunks)),
            dma((2, chunks)), dma((2,)), dma((2, chunks)),
        ],
        compiler_params=pltpu.CompilerParams(
            collective_id=0, has_side_effects=True, vmem_limit_bytes=VMEM_BYTES
        ),
        name="fused",
    )(
        skip_rows, skip_cols, tokens_in.reshape(tokens), gate_rows.reshape(tokens), gate,
        write_rows, read_rows, step_rows, decay_rows, norm_rows.reshape(1, features),
        write_cols, read_cols, step_cols, decay_cols,
    )
    part = BLOCK // local_cols
    out_shape, out_spec = (all_rows, local_cols, features), (part, local_cols, features)
    if local_cols == 1:
        out_shape, out_spec = (all_rows, features), (part, features)
    result = pl.pallas_call(
        functools.partial(norm_kernel, inner, per_col),
        grid=(all_rows // part,),
        out_shape=jax.ShapeDtypeStruct(out_shape, BF16),
        in_specs=[
            pl.BlockSpec((local_cols, part, features), lambda q: (0, q, 0)),
            pl.BlockSpec(squares.shape, lambda q: (0, 0)),
            pl.BlockSpec((1, features), lambda q: (0, 0)),
        ],
        out_specs=pl.BlockSpec(out_spec, lambda q: (q,) + (0,) * (len(out_spec) - 1)),
        scratch_shapes=[pltpu.VMEM((2, BLOCK, LANES), F32)],
        compiler_params=pltpu.CompilerParams(vmem_limit_bytes=VMEM_BYTES),
        name="norm",
    )(gated.reshape(local_cols, all_rows, features), squares, norm_cols.reshape(1, features))
    return result.reshape(all_rows, local_cols, features)


def solution(mesh):
    placed = (
        P("seq", None, "head"),
        P("seq", None, "head"),
        P(None, "seq", "head"),
        P(None, "seq"),
        P(None, "seq"),
        P("head", "seq"),
        P("head", "seq"),
        P("head"),
        P("head"),
        P(None, "seq"),
        P(None, "seq"),
        P("head", "seq"),
        P("head", "seq"),
        P("head"),
        P("head"),
    )
    return jax.shard_map(
        functools.partial(body, mesh.shape["seq"], mesh.shape["head"]),
        mesh=mesh, in_specs=placed, out_specs=P(None, "seq", "head"), check_vma=False,
    )
```

time: 158 us -> 125 us (0.79)
  Pallas kernels: 155 us -> 119 us
  local copies, waits for them, and re-layouts: 3.48 us -> 5.35 us
    pallas_call x7 -> x1, Pallas kernels: 148 us -> 113 us  [body(): pl.pallas_call(functools.partial(fused_kernel, seq, head, inner, grid_col...]
    unnamed x7 -> x5, local copies, waits for them, and re-layouts: 2.29 us -> 4.15 us
where the time goes in v1:
time: 125 us; the launch traced here: 124 us
  Pallas kernels  119 us (95%)
  local copies, waits for them, and re-layouts  5.35 us (4%)
    pallas_call x1, Pallas kernels, body(): pl.pallas_call(functools.partial(fused_kernel, seq, head, inner, grid_col...  113 us
    pallas_call x1, Pallas kernels, body(): pl.pallas_call(functools.partial(norm_kernel, inner, per_col), grid=(all_...  6.16 us
    unnamed x5, local copies, waits for them, and re-layouts  4.15 us

profile of v1, /device:TPU:25, one launch (start us, length us, event | category | flops | bytes accessed | tf_op | source)
XLA Modules:
  0.0 124.5 jit_solution(7529193623197181808)
XLA Ops:
  0.0 0.0 copy-start
  0.0 4.1 %copy.18 = bf16[256,4,1536]{2,0,1:T(8,128)(2,1)} copy(bf16[256,4,1536]{2,1,0:T(4,128)(2,1)} %param.17) | data formatting | bytes 6291456 | tf_op args[2]
  4.1 0.0 copy-done
  4.1 0.6 reshape.14.gain1
  4.7 0.0 copy-start.1
  4.7 112.9 %fused.1 = (bf16[4,256,1536]{2,1,0:T(8,128)(2,1)}, f32[8,256]{1,0:T(8,128)}) custom-call(f32[12]{0:T(128)} %skip1.1, f32[12]{0:T(128)} %skip2.1, bf16[4,256,1536]{2,1,0:T(8,128)(2,1)} %bitcast.6, bf16[4,256,1536]{2,1,0:T(8,128)(2,1)} %bitcast.7, bf16[4,256,1536]{2,1,0:T(8,128)(2,1)} %bitcast.5, bf16[64,1024]{1,0:T(8,128)(2,1)} %write1.1, ...), custom_call_target="tpu_custom_call" | custom-call | tf_op jit(solution)/shard_map/fused/pallas_call | solution.py:593
  117.7 0.0 copy-done.1
  117.7 0.6 reshape.15.gain_ref
  118.3 6.2 %norm.1 = bf16[256,4,1536]{2,1,0:T(4,128)(2,1)} custom-call(bf16[4,256,1536]{2,1,0:T(8,128)(2,1)} %get-tuple-element.7.gated_ref, f32[8,256]{1,0:T(8,128)} %get-tuple-element.8.squares_ref, f32[1,1536]{1,0:T(1,128)} %reshape.15.gain_ref), custom_call_target="tpu_custom_call" | custom-call | tf_op jit(solution)/shard_map/norm/pallas_call | solution.py:634
Async XLA Ops:
  0.0 4.1 %copy-start = (f32[1536]{0:T(1024)S(1)}, f32[1536]{0:T(1024)}, u32[]{:S(2)}) copy-start(f32[1536]{0:T(1024)} %param.23) | copy-start | bytes 18436
  4.7 112.9 %copy-start.1 = (f32[1536]{0:T(1024)S(1)}, f32[1536]{0:T(1024)}, u32[]{:S(2)}) copy-start(f32[1536]{0:T(1024)} %param.29) | copy-start | bytes 18436

commit v2 on v1

--- a/solution.py
+++ b/solution.py
@@ -10,6 +10,8 @@
 HALF = 128
 LANES = 128
 CHUNK = 2
+SMALL = 9
+STAGGER = 3
 EPSILON = 1e-05
 LOG2E = 1.4426950408889634
 HIGHEST = lax.Precision.HIGHEST
@@ -276,16 +278,20 @@
 
 def fused_kernel(
     seq, head_count, inner, grid_cols, local_cols, per_col,
-    skip1, skip2, x_hbm, gate1_hbm, gate2_hbm, write1, read1, step1, decay1, gain1,
-    write2, read2, step2, decay2,
-    out_hbm, total_ref,
-    x, gate1, gate2, sendbuf, recvbuf, hidden, outbuf, innerbuf, turned,
+    skip1, skip2, x_hbm, gate1_hbm, gate2_hbm, *refs
+):
+    small_hbm, refs = refs[:SMALL], refs[SMALL:]
+    out_hbm, scale_ref, x, gate1, gate2, sendbuf, recvbuf, hidden, innerbuf, turned, *refs = refs
+    small, refs = refs[:SMALL], refs[SMALL:]
+    decay1, step1, write1, read1, gain1, decay2, step2, write2, read2 = small
+    (
+        gate_raw, outbuf, woven,
     stage, cum1, cum2, weights, fades1, fades2, before1, before2, total1, total2, across, lifting,
     scores, read_t, state, local, prior, squares, rows1, held1, held2, scale, scales, column,
     sent1, swapped1, passed1, came1, near1, sent2, swapped2, passed2, came2, near2,
-    load_sems, bulk_send, bulk_recv, keep_sems, sum1, sum2, scale_send, scale_recv, out_sems,
+    load_sems, small_sems, bulk_send, bulk_recv, keep_sems, sum1, sum2, scale_send, scale_recv, out_sems,
     swap1_sems, near1_sems, pass1_sems, swap2_sems, near2_sems, pass2_sems,
-):
+    ) = refs
     axes = (("seq", seq), ("head", head_count))
     me = lax.axis_index("seq")
     blocks, _, features = x.shape
@@ -303,11 +309,19 @@
 
     gate_loads = [
         pltpu.make_async_copy(gate1_hbm, gate1, load_sems.at[1, 0]),
-        pltpu.make_async_copy(gate2_hbm, gate2, load_sems.at[2, 0]),
+        pltpu.make_async_copy(
+            gate2_hbm, gate_raw if local_cols > 1 else gate2, load_sems.at[2, 0]
+        ),
     ]
+    small_loads = [
+        pltpu.make_async_copy(source, target, small_sems.at[i])
+        for i, (source, target) in enumerate(zip(small_hbm, small))
+    ]
+    for copy in small_loads[:3]:
+        copy.start()
     for b in range(blocks):
         load(b).start()
-    for copy in gate_loads:
+    for copy in small_loads[3:] + gate_loads:
         copy.start()
 
     shared = dict(
@@ -334,7 +348,10 @@
         came1[...] = jnp.zeros_like(came1)
         came2[...] = jnp.zeros_like(came2)
 
+    for copy in small_loads[:2]:
+        copy.wait()
     prepare_sums(one)
+    small_loads[2].wait()
     state[...] = jnp.zeros_like(state)
 
     def states1(b, carry):
@@ -350,6 +367,7 @@
     for c, part in enumerate(parts):
         ex1.swap(c, part)
 
+    small_loads[3].wait()
     prepare_scores(one)
     squares[...] = jnp.zeros_like(squares)
 
@@ -402,8 +420,7 @@
 
     inner1(0)
     fades = ex1.fades()
-    for copy in gate_loads:
-        copy.wait()
+    gate_loads[0].wait()
     ex1.step(0, parts[0], fades)
     finish1(0)
     for hop in range(1, seq):
@@ -412,8 +429,13 @@
         def _(hop=hop):
             bulk(0, hop).start()
 
-    for c in range(1, chunks):
-        ex1.step(c, parts[c], fades)
+    soon = ex1.group < ex1.groups // 2
+
+    @pl.when(soon)
+    def _():
+        for c in range(1, chunks):
+            ex1.step(c, parts[c], fades)
+
     for hop in range(1, seq):
 
         @pl.when(hop > me)
@@ -423,6 +445,11 @@
     keep(0).start()
     for c in range(1, chunks):
         inner1(c)
+
+        @pl.when(jnp.logical_not(soon))
+        def _(c=c):
+            ex1.step(c, parts[c], fades)
+
         finish1(c)
         if c == 1:
             send_all(c)
@@ -446,11 +473,26 @@
         send_all(c)
     scales[mine, :] = scale[...]
 
+    for copy in small_loads[4:]:
+        copy.wait()
     prepare_sums(two)
     prepare_scores(two)
     state[...] = jnp.zeros_like(state)
     squares[...] = jnp.zeros_like(squares)
     ex2.near_copy().start()
+    gate_loads[1].wait()
+    all_rows = per_col * BLOCK
+
+    def place_of(b):
+        return pl.ds(lax.rem(b, per_col) * (BLOCK * local_cols) + b // per_col, BLOCK, stride=local_cols)
+
+    if local_cols > 1:
+        for h in range(heads):
+            slot = woven.at[h % 2]
+            slot[...] = gate_raw[:, :, lanes_of(h)].astype(F32).reshape(all_rows * local_cols, LANES)
+            for b in range(blocks):
+                at = (b % per_col) * BLOCK * local_cols + b // per_col
+                gate2[b, :, lanes_of(h)] = slot[pl.ds(at, BLOCK, stride=local_cols), :].astype(BF16)
     for copy in scale_copies:
         copy.wait()
 
@@ -476,7 +518,7 @@
             for h in numbers[c]:
                 lanes = lanes_of(h)
                 own = recvbuf[slab, b // per_col, :, :, lanes].astype(F32).reshape(BLOCK, LANES)
-                own = (own * column[b] * gain1[:, lanes]).astype(BF16)
+                own = (own * column[b] * gain1[h : h + 1, :]).astype(BF16)
                 hidden[b, :, lanes] = own
                 add_state(two, b, h, write32, own)
             return carry
@@ -492,12 +534,14 @@
         lax.fori_loop(0, blocks, block, 0)
 
     def store2(b, h, gated):
-        outbuf[b, :, lanes_of(h)] = gated.astype(BF16)
+        if local_cols > 1:
+            woven[h % CHUNK, place_of(b), :] = gated
+        else:
+            outbuf[pl.ds(pl.multiple_of(b * BLOCK, BLOCK), BLOCK), lanes_of(h)] = gated.astype(BF16)
 
     def put(c):
-        return pltpu.make_async_copy(
-            outbuf.at[:, :, wide(c)], out_hbm.at[:, :, wide(c)], out_sems.at[c]
-        )
+        span = (slice(None),) * (len(outbuf.shape) - 1) + (wide(c),)
+        return pltpu.make_async_copy(outbuf.at[span], out_hbm.at[span], out_sems.at[c])
 
     def finish2(c):
         def block(b, carry):
@@ -505,59 +549,58 @@
             return carry
 
         lax.fori_loop(0, blocks, block, 0)
+        if local_cols > 1:
+            for h in numbers[c]:
+                outbuf[:, :, lanes_of(h)] = (
+                    woven[h % CHUNK].reshape(all_rows, local_cols, LANES).astype(BF16)
+                )
         put(c).start()
 
-    last = chunks - 1
-    early = max(last - 1, 0)
-    fades = None
+    lag = jnp.minimum(ex2.group, STAGGER)
+    fades = ex2.fades()
+
+    def chain(slot):
+        for late in range(STAGGER + 1):
+            c = slot - 1 - late
+            if 0 <= c < chunks:
+
+                @pl.when(lag == late)
+                def _(c=c):
+                    ex2.step(c, parts[c], fades)
+
     for c in range(chunks):
-        if c == last and last > 0:
-            fades = ex2.fades()
-            for e in range(early):
-                ex2.step(e, parts[e], fades)
-            for e in range(early):
-                finish2(e)
         arrive(c)
         states2(c)
         ex2.swap(c, parts[c])
-        if c < last:
-            inner2(c)
-    if fades is None:
-        fades = ex2.fades()
-    for c in range(early, last):
-        ex2.step(c, parts[c], fades)
-    inner2(last)
-    ex2.step(last, parts[last], fades)
-    for c in range(early, chunks):
-        finish2(c)
+        inner2(c)
+        chain(c)
+    done = 0
+    for slot in range(chunks, chunks + STAGGER + 1):
+        chain(slot)
+        while done < slot - STAGGER - 1 or (slot == chunks + STAGGER and done < chunks):
+            finish2(done)
+            done += 1
     reduce_squares(two, rows1)
-    total_ref[...] = head_sum(head_count, rows1, held2, sum2.at[0], sum2.at[1])
+    total = head_sum(head_count, rows1, held2, sum2.at[0], sum2.at[1])
+    total = jnp.transpose(lax.rsqrt(total / inner + EPSILON))
+    for b in range(blocks):
+        at = (b % per_col) * BLOCK * local_cols + b // per_col
+        scale_ref[pl.ds(at, BLOCK, stride=local_cols), :] = jnp.broadcast_to(
+            total[:, b : b + 1], (BLOCK, LANES)
+        )
     for c in range(chunks):
         put(c).wait()
     ex1.settle(parts)
     ex2.settle(parts)
 
 
-def norm_kernel(inner, per_col, gated_ref, squares_ref, gain_ref, out_ref, turned):
-    cols, rows, features = gated_ref.shape
-    square = (BLOCK, BLOCK)
-    start = pl.program_id(0) * rows
-    lane = start % BLOCK + iota(square, 0) % rows
-    sums = contract((lane == iota(square, 1)).astype(F32), squares_ref[...], ((1,), (1,)), HIGHEST)
-    block = (iota(sums.shape, 0) // rows) * per_col + start // BLOCK
-    sums = jnp.sum(jnp.where(iota(sums.shape, 1) == block, sums, 0.0), axis=1, keepdims=True)
-    scaled = lax.rsqrt(sums / inner + EPSILON)
-    for at in range(0, features, LANES):
-        lanes = slice(at, at + LANES)
-        gated = gated_ref[:, :, lanes].astype(F32).reshape(BLOCK, LANES)
-        result = gated * scaled * gain_ref[:, lanes]
-        if cols > 1:
-            slot = turned.at[at // LANES % 2]
-            for c in range(cols):
-                slot[pl.ds(c, rows, stride=cols), :] = result[c * rows : (c + 1) * rows]
-            out_ref[:, :, lanes] = slot[...].reshape(rows, cols, LANES).astype(BF16)
-        else:
-            out_ref[:, lanes] = result.astype(BF16)
+def norm_kernel(gated_ref, scale_ref, gain_ref, out_ref):
+    shape = gated_ref.shape[:-1] + (LANES,)
+    scale = scale_ref[...].reshape(shape)
+    for h in range(gated_ref.shape[-1] // LANES):
+        lanes = lanes_of(h)
+        gated = gated_ref[..., lanes].astype(F32)
+        out_ref[..., lanes] = (gated * scale * gain_ref[h : h + 1, :]).astype(BF16)
 
 
 def body(
@@ -589,19 +632,28 @@
     tall = (blocks, BLOCK, padded)
     states = (heads, size, width)
     exchange = [vmem(states, BF16)] * 4 + [vmem(total, F32)]
-    gate = jnp.transpose(gate_cols, (1, 0, 2)).reshape(tokens)
-    gated, squares = pl.pallas_call(
+    small = (
+        decay_rows, step_rows, write_rows, read_rows, norm_rows.reshape(heads, width),
+        decay_cols, step_cols, write_cols, read_cols,
+    )
+    raw = (all_rows, local_cols, features)
+    flat = raw if local_cols > 1 else (all_rows, features)
+    gate = gate_cols if local_cols > 1 else gate_cols.reshape(tokens)
+    gated, scale = pl.pallas_call(
         functools.partial(fused_kernel, seq, head, inner, grid_cols, local_cols, per_col),
         out_shape=(
-            jax.ShapeDtypeStruct(tokens, BF16),
-            jax.ShapeDtypeStruct((depth, BLOCK), F32),
+            jax.ShapeDtypeStruct(flat, BF16),
+            jax.ShapeDtypeStruct((all_rows * local_cols, LANES), F32),
         ),
-        in_specs=[smem, smem] + [anywhere] * 3 + [whole] * 9,
+        in_specs=[smem, smem] + [anywhere] * (3 + SMALL),
         out_specs=(anywhere, whole),
         scratch_shapes=[
             vmem(tokens, BF16), vmem(tokens, BF16), vmem(tokens, BF16),
-            vmem(packed, BF16), vmem(packed, BF16), vmem(tokens, BF16), vmem(tokens, BF16),
+            vmem(packed, BF16), vmem(packed, BF16), vmem(tokens, BF16),
             vmem(tokens, F32), vmem((2, BLOCK, LANES), F32),
+            *(vmem(array.shape, array.dtype) for array in small),
+            vmem(raw if local_cols > 1 else (1, LANES), BF16), vmem(flat, BF16),
+            vmem((CHUNK, all_rows * local_cols if local_cols > 1 else 8, LANES), F32),
             vmem((blocks, 3, padded, BLOCK), BF16), vmem(sums, F32), vmem(sums, F32),
             vmem(sums, F32), vmem(rows, F32), vmem(rows, F32), vmem(rows, F32), vmem(rows, F32),
             vmem(total, F32), vmem(total, F32), vmem(tall, F32), vmem(tall, F32),
@@ -612,7 +664,7 @@
             vmem((depth, BLOCK), F32), vmem((seq * depth, BLOCK), F32),
             vmem((blocks, BLOCK, LANES), F32),
             *exchange, *exchange,
-            dma((3, blocks)), dma((seq - 1, chunks)), dma((seq - 1, chunks)), dma((chunks,)),
+            dma((3, blocks)), dma((SMALL,)), dma((seq - 1, chunks)), dma((seq - 1, chunks)), dma((chunks,)),
             dma((2, head - 1)), dma((2, head - 1)), dma((seq - 1,)), dma((seq - 1,)),
             dma((chunks,)),
             dma((2, chunks)), dma((2,)), dma((2, chunks)),
@@ -623,28 +675,24 @@
         ),
         name="fused",
     )(
-        skip_rows, skip_cols, tokens_in.reshape(tokens), gate_rows.reshape(tokens), gate,
-        write_rows, read_rows, step_rows, decay_rows, norm_rows.reshape(1, features),
-        write_cols, read_cols, step_cols, decay_cols,
-    )
-    part = BLOCK // local_cols
-    out_shape, out_spec = (all_rows, local_cols, features), (part, local_cols, features)
-    if local_cols == 1:
-        out_shape, out_spec = (all_rows, features), (part, features)
+        skip_rows, skip_cols, tokens_in.reshape(tokens), gate_rows.reshape(tokens), gate, *small
+    )
+    part = min(all_rows, BLOCK // local_cols // 2)
+    block = (part,) + flat[1:]
+    spec = pl.BlockSpec(block, lambda q: (q,) + (0,) * (len(block) - 1))
     result = pl.pallas_call(
-        functools.partial(norm_kernel, inner, per_col),
+        norm_kernel,
         grid=(all_rows // part,),
-        out_shape=jax.ShapeDtypeStruct(out_shape, BF16),
+        out_shape=jax.ShapeDtypeStruct(flat, BF16),
         in_specs=[
-            pl.BlockSpec((local_cols, part, features), lambda q: (0, q, 0)),
-            pl.BlockSpec(squares.shape, lambda q: (0, 0)),
-            pl.BlockSpec((1, features), lambda q: (0, 0)),
+            spec,
+            pl.BlockSpec((part * local_cols, LANES), lambda q: (q, 0)),
+            pl.BlockSpec((heads, width), lambda q: (0, 0)),
         ],
-        out_specs=pl.BlockSpec(out_spec, lambda q: (q,) + (0,) * (len(out_spec) - 1)),
-        scratch_shapes=[pltpu.VMEM((2, BLOCK, LANES), F32)],
+        out_specs=spec,
         compiler_params=pltpu.CompilerParams(vmem_limit_bytes=VMEM_BYTES),
         name="norm",
-    )(gated.reshape(local_cols, all_rows, features), squares, norm_cols.reshape(1, features))
+    )(gated, scale, norm_cols.reshape(heads, width))
     return result.reshape(all_rows, local_cols, features)
 
 

time: 125 us -> 112 us (0.90)
  Pallas kernels: 119 us -> 112 us
  local copies, waits for them, and re-layouts: 5.35 us -> 0 us
    pallas_call x1, Pallas kernels: 113 us -> 105 us  [body(): pl.pallas_call(functools.partial(fused_kernel, seq, head, inner, grid_col...]
    unnamed x5 -> x0, local copies, waits for them, and re-layouts: 4.15 us -> none
where the time goes in v2:
time: 112 us
  Pallas kernels  112 us (100%)
    pallas_call x1, Pallas kernels, body(): pl.pallas_call(functools.partial(fused_kernel, seq, head, inner, grid_col...  105 us
    pallas_call x1, Pallas kernels, body(): pl.pallas_call(norm_kernel, grid=(all_rows // part,), out_shape=jax.Shape...  6.82 us

profile of v2, /device:TPU:25, one launch (start us, length us, event | category | flops | bytes accessed | tf_op | source)
XLA Modules:
  0.0 112.1 jit_solution(7306559053601072805)
XLA Ops:
  0.0 105.3 %fused.1 = (bf16[256,4,1536]{2,1,0:T(4,128)(2,1)}, f32[1024,128]{1,0:T(8,128)}) custom-call(f32[12]{0:T(128)} %skip1.1, f32[12]{0:T(128)} %skip2.1, bf16[4,256,1536]{2,1,0:T(8,128)(2,1)} %bitcast.4, bf16[4,256,1536]{2,1,0:T(8,128)(2,1)} %bitcast.5, bf16[256,4,1536]{2,1,0:T(4,128)(2,1)} %gate2_hbm.1, f32[12,1024]{1,0:T(8,128)} %refs_0_.1, ...), custom_call_target="tpu_custom_call" | custom-call | tf_op jit(solution)/shard_map/fused/pallas_call | solution.py:642
  105.3 6.8 %norm.1 = bf16[256,4,1536]{2,1,0:T(4,128)(2,1)} custom-call(bf16[256,4,1536]{2,1,0:T(4,128)(2,1)} %get-tuple-element.7.gated_ref, f32[1024,128]{1,0:T(8,128)} %get-tuple-element.8.scale_ref, f32[12,128]{1,0:T(8,128)} %bitcast.7), custom_call_target="tpu_custom_call" | custom-call | tf_op jit(solution)/shard_map/norm/pallas_call | solution.py:683

commit v3 on v2

--- a/solution.py
+++ b/solution.py
@@ -11,7 +11,6 @@
 LANES = 128
 CHUNK = 2
 SMALL = 9
-STAGGER = 3
 EPSILON = 1e-05
 LOG2E = 1.4426950408889634
 HIGHEST = lax.Precision.HIGHEST
@@ -138,11 +137,15 @@
     for i, h in enumerate(hs):
         out = layer.inner[b, :, lanes_of(h)]
         out += layer.lifting[b, :, h : h + 1] * from_state[:, i * LANES : (i + 1) * LANES]
-        gate = layer.gate[b, :, lanes_of(h)].astype(F32)
-        gated = out * (gate / (1.0 + jnp.exp2(gate * -LOG2E)))
+        gated = out * layer.silu[b, :, lanes_of(h)]
         squares += gated * gated
         store(b, h, gated)
     layer.squares[b] += squares
+
+
+def silu(gate):
+    gate = gate.astype(F32)
+    return gate / (1.0 + jnp.exp2(gate * -LOG2E))
 
 
 def reduce_squares(layer, rows_ref):
@@ -204,10 +207,12 @@
 
 
 class Exchange:
-    def __init__(self, seq, layer, sent, swapped, passed, came, near, swap_sems, near_sems, pass_sems):
-        self.layer, self.sent, self.swapped = layer, sent, swapped
-        self.passed, self.came, self.near = passed, came, near
-        self.swap_sems, self.near_sems, self.pass_sems = swap_sems, near_sems, pass_sems
+    def __init__(self, seq, layer, refs, sems):
+        self.layer = layer
+        self.sent, self.swapped, self.passed, self.came, self.near, *refs = refs
+        self.own, self.landed, self.pair_total, self.pair_totals, self.span = refs
+        self.swap_sems, self.near_sems, self.pass_sems, self.own_sems, self.total_sems = sems
+        self.seq, self.me = seq, lax.axis_index("seq")
         me = lax.axis_index("seq")
         self.place = lax.rem(me, 2)
         self.partner = me + 1 - 2 * self.place
@@ -257,8 +262,7 @@
             self.pass_copy(c, part).wait_recv()
 
         for h in range(part.start, part.start + part.size):
-            mine, other = layer.state[h], self.swapped[h].astype(F32)
-            first, last = jnp.where(even, mine, other), jnp.where(even, other, mine)
+            first, last = self.pair_of(h)
             before = self.came[h].astype(F32)
             middle = first_fade[h : h + 1] * before + first
             self.passed[h] = (last_fade[h : h + 1] * middle + last).astype(BF16)
@@ -268,12 +272,79 @@
         def _():
             self.pass_copy(c, part).start()
 
+    def own_copy(self, hop):
+        return pltpu.make_async_remote_copy(
+            src_ref=self.own, dst_ref=self.landed.at[hop - 1], send_sem=self.own_sems.at[0, hop - 1],
+            recv_sem=self.own_sems.at[1, hop - 1],
+            device_id={"seq": lax.rem(self.me + 2 * hop, self.seq)}, device_id_type=MESH,
+        )
+
+    def total_copy(self, hop):
+        return pltpu.make_async_remote_copy(
+            src_ref=self.pair_total, dst_ref=self.pair_totals.at[hop - 1],
+            send_sem=self.total_sems.at[0, hop - 1], recv_sem=self.total_sems.at[1, hop - 1],
+            device_id={"seq": lax.rem(self.me + 2 * hop, self.seq)}, device_id_type=MESH,
+        )
+
+    def announce(self):
+        self.pair_total[...] = self.layer.total[...] + self.near[...]
+        for hop in range(1, self.groups):
+
+            @pl.when(self.group + hop < self.groups)
+            def _(hop=hop):
+                self.total_copy(hop).start()
+
+    def pair_of(self, h):
+        mine, other = self.layer.state[h], self.swapped[h].astype(F32)
+        even = self.place == 0
+        return jnp.where(even, mine, other), jnp.where(even, other, mine)
+
+    def send_own(self, c, part, fades):
+        self.swap_copy(c, part).wait()
+        for i, h in enumerate(range(part.start, part.start + part.size)):
+            first, last = self.pair_of(h)
+            self.own[i] = (fades[1][h : h + 1] * first + last).astype(BF16)
+        for hop in range(1, self.groups):
+
+            @pl.when(self.group + hop < self.groups)
+            def _(hop=hop):
+                self.own_copy(hop).start()
+
+    def take_own(self, part, fades):
+        prior = self.layer.prior
+        heads = range(part.start, part.start + part.size)
+        self.span[...] = jnp.zeros_like(self.span)
+        for h in heads:
+            prior[h] = jnp.zeros(prior.shape[1:], F32)
+        for hop in range(1, self.groups):
+
+            @pl.when(self.group >= hop)
+            def _(hop=hop):
+                self.total_copy(hop).wait_recv()
+                self.own_copy(hop).wait_recv()
+                factor = jnp.exp2(self.span[...])
+                for i, h in enumerate(heads):
+                    prior[h] += factor[h : h + 1] * self.landed[hop - 1, i].astype(F32)
+                self.span[...] += self.pair_totals[hop - 1]
+
+        for h in heads:
+            before = prior[h]
+            middle = fades[0][h : h + 1] * before + self.pair_of(h)[0]
+            prior[h] = jnp.where(self.place == 0, before, middle)
+
     def settle(self, parts):
-        for c, part in enumerate(parts):
+        for c, part in parts:
 
             @pl.when(self.group < self.groups - 1)
             def _(c=c, part=part):
                 self.pass_copy(c, part).wait_send()
+
+        for hop in range(1, self.groups):
+
+            @pl.when(self.group + hop < self.groups)
+            def _(hop=hop):
+                self.total_copy(hop).wait_send()
+                self.own_copy(hop).wait_send()
 
 
 def fused_kernel(
@@ -285,13 +356,17 @@
     small, refs = refs[:SMALL], refs[SMALL:]
     decay1, step1, write1, read1, gain1, decay2, step2, write2, read2 = small
     (
-        gate_raw, outbuf, woven,
+        gate_raw, flat, woven, silus,
     stage, cum1, cum2, weights, fades1, fades2, before1, before2, total1, total2, across, lifting,
     scores, read_t, state, local, prior, squares, rows1, held1, held2, scale, scales, column,
-    sent1, swapped1, passed1, came1, near1, sent2, swapped2, passed2, came2, near2,
-    load_sems, small_sems, bulk_send, bulk_recv, keep_sems, sum1, sum2, scale_send, scale_recv, out_sems,
-    swap1_sems, near1_sems, pass1_sems, swap2_sems, near2_sems, pass2_sems,
+    *refs,
     ) = refs
+    ex1_refs, ex2_refs, refs = refs[:10], refs[10:20], refs[20:]
+    (
+        load_sems, small_sems, bulk_send, bulk_recv, keep_sems, sum1, sum2, scale_send, scale_recv,
+        out_sems, *refs,
+    ) = refs
+    ex1_sems, ex2_sems = refs[:5], refs[5:]
     axes = (("seq", seq), ("head", head_count))
     me = lax.axis_index("seq")
     blocks, _, features = x.shape
@@ -327,26 +402,23 @@
     shared = dict(
         stage=stage, weights=weights, across=across, lifting=lifting, scores=scores,
         read_t=read_t, state=state, local=local, prior=prior, squares=squares, inner=innerbuf,
+        silu=silus,
     )
     one = Layer(
-        skip=skip1, gate=gate1, write=write1, read=read1, step=step1, decay=decay1, cum=cum1,
+        skip=skip1, write=write1, read=read1, step=step1, decay=decay1, cum=cum1,
         fades=fades1, before=before1, total=total1, **shared,
     )
     two = Layer(
-        skip=skip2, gate=gate2, write=write2, read=read2, step=step2, decay=decay2, cum=cum2,
+        skip=skip2, write=write2, read=read2, step=step2, decay=decay2, cum=cum2,
         fades=fades2, before=before2, total=total2, **shared,
     )
-    ex1 = Exchange(
-        seq, one, sent1, swapped1, passed1, came1, near1, swap1_sems, near1_sems, pass1_sems
-    )
-    ex2 = Exchange(
-        seq, two, sent2, swapped2, passed2, came2, near2, swap2_sems, near2_sems, pass2_sems
-    )
+    ex1 = Exchange(seq, one, ex1_refs, ex1_sems)
+    ex2 = Exchange(seq, two, ex2_refs, ex2_sems)
 
     @pl.when(ex1.group == 0)
     def _():
-        came1[...] = jnp.zeros_like(came1)
-        came2[...] = jnp.zeros_like(came2)
+        ex1.came[...] = jnp.zeros_like(ex1.came)
+        ex2.came[...] = jnp.zeros_like(ex2.came)
 
     for copy in small_loads[:2]:
         copy.wait()
@@ -366,6 +438,9 @@
     ex1.near_copy().start()
     for c, part in enumerate(parts):
         ex1.swap(c, part)
+    fades = ex1.fades()
+    ex1.announce()
+    ex1.send_own(0, parts[0], fades)
 
     small_loads[3].wait()
     prepare_scores(one)
@@ -375,6 +450,7 @@
         def block(b, carry):
             for h in numbers[c]:
                 inner_block(one, b, h, x[b, :, lanes_of(h)])
+                silus[b, :, lanes_of(h)] = silu(gate1[b, :, lanes_of(h)])
             return carry
 
         lax.fori_loop(0, blocks, block, 0)
@@ -418,10 +494,9 @@
             bulk(c, hop).start()
         keep(c).start()
 
+    gate_loads[0].wait()
     inner1(0)
-    fades = ex1.fades()
-    gate_loads[0].wait()
-    ex1.step(0, parts[0], fades)
+    ex1.take_own(parts[0], fades)
     finish1(0)
     for hop in range(1, seq):
 
@@ -480,6 +555,8 @@
     state[...] = jnp.zeros_like(state)
     squares[...] = jnp.zeros_like(squares)
     ex2.near_copy().start()
+    ex2_fades = ex2.fades()
+    ex2.announce()
     gate_loads[1].wait()
     all_rows = per_col * BLOCK
 
@@ -492,7 +569,11 @@
             slot[...] = gate_raw[:, :, lanes_of(h)].astype(F32).reshape(all_rows * local_cols, LANES)
             for b in range(blocks):
                 at = (b % per_col) * BLOCK * local_cols + b // per_col
-                gate2[b, :, lanes_of(h)] = slot[pl.ds(at, BLOCK, stride=local_cols), :].astype(BF16)
+                silus[b, :, lanes_of(h)] = silu(slot[pl.ds(at, BLOCK, stride=local_cols), :])
+    else:
+        for h in range(heads):
+            for b in range(blocks):
+                silus[b, :, lanes_of(h)] = silu(gate2[b, :, lanes_of(h)])
     for copy in scale_copies:
         copy.wait()
 
@@ -534,14 +615,10 @@
         lax.fori_loop(0, blocks, block, 0)
 
     def store2(b, h, gated):
-        if local_cols > 1:
-            woven[h % CHUNK, place_of(b), :] = gated
-        else:
-            outbuf[pl.ds(pl.multiple_of(b * BLOCK, BLOCK), BLOCK), lanes_of(h)] = gated.astype(BF16)
+        flat[h, place_of(b), :] = gated
 
     def put(c):
-        span = (slice(None),) * (len(outbuf.shape) - 1) + (wide(c),)
-        return pltpu.make_async_copy(outbuf.at[span], out_hbm.at[span], out_sems.at[c])
+        return pltpu.make_async_copy(flat.at[parts[c]], out_hbm.at[parts[c]], out_sems.at[c])
 
     def finish2(c):
         def block(b, carry):
@@ -549,37 +626,49 @@
             return carry
 
         lax.fori_loop(0, blocks, block, 0)
-        if local_cols > 1:
-            for h in numbers[c]:
-                outbuf[:, :, lanes_of(h)] = (
-                    woven[h % CHUNK].reshape(all_rows, local_cols, LANES).astype(BF16)
-                )
         put(c).start()
 
-    lag = jnp.minimum(ex2.group, STAGGER)
-    fades = ex2.fades()
+    last = chunks - 1
+    fades = ex2_fades
 
     def chain(slot):
-        for late in range(STAGGER + 1):
+        for late in range(2):
             c = slot - 1 - late
-            if 0 <= c < chunks:
-
-                @pl.when(lag == late)
+            if 0 <= c < last:
+
+                @pl.when(soon & (jnp.minimum(ex2.group, 1) == late))
                 def _(c=c):
                     ex2.step(c, parts[c], fades)
 
     for c in range(chunks):
+        if c == last:
+            chain(last)
+            chain(last + 1)
+
+            @pl.when(soon)
+            def _():
+                for e in range(last - 1):
+                    finish2(e)
+
         arrive(c)
         states2(c)
         ex2.swap(c, parts[c])
         inner2(c)
-        chain(c)
-    done = 0
-    for slot in range(chunks, chunks + STAGGER + 1):
-        chain(slot)
-        while done < slot - STAGGER - 1 or (slot == chunks + STAGGER and done < chunks):
-            finish2(done)
-            done += 1
+        if c < last:
+            chain(c)
+    ex2.send_own(last, parts[last], fades)
+
+    @pl.when(jnp.logical_not(soon))
+    def _():
+        for e in range(last):
+            ex2.step(e, parts[e], fades)
+        for e in range(last - 1):
+            finish2(e)
+
+    if last > 0:
+        finish2(last - 1)
+    ex2.take_own(parts[last], fades)
+    finish2(last)
     reduce_squares(two, rows1)
     total = head_sum(head_count, rows1, held2, sum2.at[0], sum2.at[1])
     total = jnp.transpose(lax.rsqrt(total / inner + EPSILON))
@@ -590,17 +679,45 @@
         )
     for c in range(chunks):
         put(c).wait()
-    ex1.settle(parts)
-    ex2.settle(parts)
-
-
-def norm_kernel(gated_ref, scale_ref, gain_ref, out_ref):
-    shape = gated_ref.shape[:-1] + (LANES,)
-    scale = scale_ref[...].reshape(shape)
-    for h in range(gated_ref.shape[-1] // LANES):
-        lanes = lanes_of(h)
-        gated = gated_ref[..., lanes].astype(F32)
-        out_ref[..., lanes] = (gated * scale * gain_ref[h : h + 1, :]).astype(BF16)
+    numbered = list(enumerate(parts))
+    ex1.settle(numbered[1:])
+    ex2.settle(numbered[:-1])
+
+
+def norm_kernel(steps, gated_hbm, scale_hbm, gain_ref, out_hbm, gated, scale, out, load_sems, out_sems):
+    heads, rows, _ = gated.shape
+    part = rows // steps
+    tall = out.shape[0] // steps
+    loads = [
+        pltpu.make_async_copy(scale_hbm, scale, load_sems.at[steps]),
+        *(
+            pltpu.make_async_copy(
+                gated_hbm.at[:, pl.ds(i * part, part)], gated.at[:, pl.ds(i * part, part)],
+                load_sems.at[i],
+            )
+            for i in range(steps)
+        ),
+    ]
+    puts = [
+        pltpu.make_async_copy(
+            out.at[pl.ds(i * tall, tall)], out_hbm.at[pl.ds(i * tall, tall)], out_sems.at[i]
+        )
+        for i in range(steps)
+    ]
+    for copy in loads:
+        copy.start()
+    loads[0].wait()
+    for i in range(steps):
+        loads[i + 1].wait()
+        span = pl.ds(i * part, part)
+        for h in range(heads):
+            lanes = lanes_of(h)
+            result = gated[h, span, :] * scale[span, :] * gain_ref[h : h + 1, :]
+            shape = (tall,) + out.shape[1:-1] + (LANES,)
+            out[pl.ds(i * tall, tall), ..., lanes] = result.reshape(shape).astype(BF16)
+        puts[i].start()
+    for copy in puts:
+        copy.wait()
 
 
 def body(
@@ -631,7 +748,14 @@
     total = (padded, LANES)
     tall = (blocks, BLOCK, padded)
     states = (heads, size, width)
-    exchange = [vmem(states, BF16)] * 4 + [vmem(total, F32)]
+    groups = seq // 2
+    held = (min(CHUNK, heads), size, width)
+    far = max(groups - 1, 1)
+    exchange = [vmem(states, BF16)] * 4 + [
+        vmem(total, F32), vmem(held, BF16), vmem((far,) + held, BF16), vmem(total, F32),
+        vmem((far,) + total, F32), vmem(total, F32),
+    ]
+    exchange_sems = [dma((2, chunks)), dma((2,)), dma((2, chunks)), dma((2, far)), dma((2, far))]
     small = (
         decay_rows, step_rows, write_rows, read_rows, norm_rows.reshape(heads, width),
         decay_cols, step_cols, write_cols, read_cols,
@@ -642,18 +766,21 @@
     gated, scale = pl.pallas_call(
         functools.partial(fused_kernel, seq, head, inner, grid_cols, local_cols, per_col),
         out_shape=(
-            jax.ShapeDtypeStruct(flat, BF16),
+            jax.ShapeDtypeStruct((heads, all_rows * local_cols, LANES), F32),
             jax.ShapeDtypeStruct((all_rows * local_cols, LANES), F32),
         ),
         in_specs=[smem, smem] + [anywhere] * (3 + SMALL),
         out_specs=(anywhere, whole),
         scratch_shapes=[
-            vmem(tokens, BF16), vmem(tokens, BF16), vmem(tokens, BF16),
+            vmem(tokens, BF16), vmem(tokens, BF16),
+            vmem(tokens if local_cols == 1 else (1, BLOCK, LANES), BF16),
             vmem(packed, BF16), vmem(packed, BF16), vmem(tokens, BF16),
             vmem(tokens, F32), vmem((2, BLOCK, LANES), F32),
             *(vmem(array.shape, array.dtype) for array in small),
-            vmem(raw if local_cols > 1 else (1, LANES), BF16), vmem(flat, BF16),
-            vmem((CHUNK, all_rows * local_cols if local_cols > 1 else 8, LANES), F32),
+            vmem(raw if local_cols > 1 else (1, LANES), BF16),
+            vmem((heads, all_rows * local_cols, LANES), F32),
+            vmem((2, all_rows * local_cols if local_cols > 1 else 8, LANES), F32),
+            vmem(tokens, F32),
             vmem((blocks, 3, padded, BLOCK), BF16), vmem(sums, F32), vmem(sums, F32),
             vmem(sums, F32), vmem(rows, F32), vmem(rows, F32), vmem(rows, F32), vmem(rows, F32),
             vmem(total, F32), vmem(total, F32), vmem(tall, F32), vmem(tall, F32),
@@ -667,8 +794,7 @@
             dma((3, blocks)), dma((SMALL,)), dma((seq - 1, chunks)), dma((seq - 1, chunks)), dma((chunks,)),
             dma((2, head - 1)), dma((2, head - 1)), dma((seq - 1,)), dma((seq - 1,)),
             dma((chunks,)),
-            dma((2, chunks)), dma((2,)), dma((2, chunks)),
-            dma((2, chunks)), dma((2,)), dma((2, chunks)),
+            *exchange_sems, *exchange_sems,
         ],
         compiler_params=pltpu.CompilerParams(
             collective_id=0, has_side_effects=True, vmem_limit_bytes=VMEM_BYTES
@@ -677,19 +803,16 @@
     )(
         skip_rows, skip_cols, tokens_in.reshape(tokens), gate_rows.reshape(tokens), gate, *small
     )
-    part = min(all_rows, BLOCK // local_cols // 2)
-    block = (part,) + flat[1:]
-    spec = pl.BlockSpec(block, lambda q: (q,) + (0,) * (len(block) - 1))
+    steps = 8
     result = pl.pallas_call(
-        norm_kernel,
-        grid=(all_rows // part,),
+        functools.partial(norm_kernel, steps),
         out_shape=jax.ShapeDtypeStruct(flat, BF16),
-        in_specs=[
-            spec,
-            pl.BlockSpec((part * local_cols, LANES), lambda q: (q, 0)),
-            pl.BlockSpec((heads, width), lambda q: (0, 0)),
+        in_specs=[anywhere, anywhere, whole],
+        out_specs=anywhere,
+        scratch_shapes=[
+            vmem(gated.shape, F32), vmem(scale.shape, F32), vmem(flat, BF16),
+            dma((steps + 1,)), dma((steps,)),
         ],
-        out_specs=spec,
         compiler_params=pltpu.CompilerParams(vmem_limit_bytes=VMEM_BYTES),
         name="norm",
     )(gated, scale, norm_cols.reshape(heads, width))

time: 112 us -> 114 us (1.018); the launches traced: 112 us -> 113 us
    pallas_call x1, Pallas kernels: 105 us -> 107 us  [body(): pl.pallas_call(functools.partial(fused_kernel, seq, head, inner, grid_col...]
    pallas_call x1, Pallas kernels: 6.82 us -> 5.39 us  [body(): pl.pallas_call(functools.partial(norm_kernel, steps), out_shape=jax.Shape...]
where the time goes in v3:
time: 114 us; the launch traced here: 113 us
  Pallas kernels  112 us (98%)
    pallas_call x1, Pallas kernels, body(): pl.pallas_call(functools.partial(fused_kernel, seq, head, inner, grid_col...  107 us
    pallas_call x1, Pallas kernels, body(): pl.pallas_call(functools.partial(norm_kernel, steps), out_shape=jax.Shape...  5.39 us

profile of v3, /device:TPU:25, one launch (start us, length us, event | category | flops | bytes accessed | tf_op | source)
XLA Modules:
  0.0 112.6 jit_solution(9777685949459532751)
XLA Ops:
  0.0 107.0 %fused.1 = (f32[12,1024,128]{2,1,0:T(8,128)}, f32[1024,128]{1,0:T(8,128)}) custom-call(f32[12]{0:T(128)} %skip1.1, f32[12]{0:T(128)} %skip2.1, bf16[4,256,1536]{2,1,0:T(8,128)(2,1)} %bitcast.4, bf16[4,256,1536]{2,1,0:T(8,128)(2,1)} %bitcast.5, bf16[256,4,1536]{2,1,0:T(4,128)(2,1)} %gate2_hbm.1, f32[12,1024]{1,0:T(8,128)} %refs_0_.1, f32[12,1024]{1,0:T(8,128)} %refs_1_.1, ...), custom_call_target="tpu_custom_call" | custom-call | tf_op jit(solution)/shard_map/fused/pallas_call | solution.py:766
  107.0 5.4 %norm.1 = bf16[256,4,1536]{2,1,0:T(4,128)(2,1)} custom-call(f32[12,1024,128]{2,1,0:T(8,128)} %get-tuple-element.7.gated_hbm, f32[1024,128]{1,0:T(8,128)} %get-tuple-element.8.scale_hbm, f32[12,128]{1,0:T(8,128)} %bitcast.7), custom_call_target="tpu_custom_call" | custom-call | tf_op jit(solution)/shard_map/norm/pallas_call | solution.py:807

commit v4 on v3

--- a/solution.py
+++ b/solution.py
@@ -434,6 +434,20 @@
         return carry
 
     lax.fori_loop(0, blocks, states1, 0)
+    def inner1(c):
+        def block(b, carry):
+            for h in numbers[c]:
+                inner_block(one, b, h, x[b, :, lanes_of(h)])
+                silus[b, :, lanes_of(h)] = silu(gate1[b, :, lanes_of(h)])
+            return carry
+
+        lax.fori_loop(0, blocks, block, 0)
+
+    small_loads[3].wait()
+    prepare_scores(one)
+    squares[...] = jnp.zeros_like(squares)
+    gate_loads[0].wait()
+    inner1(0)
     greet_wait(axes)
     ex1.near_copy().start()
     for c, part in enumerate(parts):
@@ -441,19 +455,12 @@
     fades = ex1.fades()
     ex1.announce()
     ex1.send_own(0, parts[0], fades)
-
-    small_loads[3].wait()
-    prepare_scores(one)
-    squares[...] = jnp.zeros_like(squares)
-
-    def inner1(c):
-        def block(b, carry):
-            for h in numbers[c]:
-                inner_block(one, b, h, x[b, :, lanes_of(h)])
-                silus[b, :, lanes_of(h)] = silu(gate1[b, :, lanes_of(h)])
-            return carry
-
-        lax.fori_loop(0, blocks, block, 0)
+    soon = ex1.group < ex1.groups // 2
+
+    @pl.when(ex1.group == 0)
+    def _():
+        for c in range(1, chunks):
+            ex1.step(c, parts[c], fades)
 
     def store1(b, h, gated):
         slot = turned.at[h % 2]
@@ -494,8 +501,6 @@
             bulk(c, hop).start()
         keep(c).start()
 
-    gate_loads[0].wait()
-    inner1(0)
     ex1.take_own(parts[0], fades)
     finish1(0)
     for hop in range(1, seq):
@@ -504,9 +509,8 @@
         def _(hop=hop):
             bulk(0, hop).start()
 
-    soon = ex1.group < ex1.groups // 2
-
-    @pl.when(soon)
+
+    @pl.when(soon & (ex1.group > 0))
     def _():
         for c in range(1, chunks):
             ex1.step(c, parts[c], fades)
@@ -644,10 +648,11 @@
         if c == last:
             chain(last)
             chain(last + 1)
+        if c == last - 1:
 
             @pl.when(soon)
             def _():
-                for e in range(last - 1):
+                for e in range(last - 3):
                     finish2(e)
 
         arrive(c)
@@ -656,17 +661,28 @@
         inner2(c)
         if c < last:
             chain(c)
-    ex2.send_own(last, parts[last], fades)
-
-    @pl.when(jnp.logical_not(soon))
+    ends = ex2.group == ex2.groups - 1
+
+    @pl.when(jnp.logical_not(soon | ends))
     def _():
         for e in range(last):
             ex2.step(e, parts[e], fades)
-        for e in range(last - 1):
+
+    ex2.send_own(last, parts[last], fades)
+    for e in range(last):
+
+        @pl.when(ends)
+        def _(e=e):
+            ex2.step(e, parts[e], fades)
+
+        if e < last - 3:
+
+            @pl.when(jnp.logical_not(soon))
+            def _(e=e):
+                finish2(e)
+
+        else:
             finish2(e)
-
-    if last > 0:
-        finish2(last - 1)
     ex2.take_own(parts[last], fades)
     finish2(last)
     reduce_squares(two, rows1)

time: 114 us -> 110 us (0.965); the launches traced: 113 us -> 110 us
  Pallas kernels: 112 us -> 110 us
    pallas_call x1, Pallas kernels: 107 us -> 104 us  [body(): pl.pallas_call(functools.partial(fused_kernel, seq, head, inner, grid_col...]
where the time goes in v4:
time: 110 us
  Pallas kernels  110 us (100%)
    pallas_call x1, Pallas kernels, body(): pl.pallas_call(functools.partial(fused_kernel, seq, head, inner, grid_col...  104 us
    pallas_call x1, Pallas kernels, body(): pl.pallas_call(functools.partial(norm_kernel, steps), out_shape=jax.Shape...  5.39 us

profile of v4, /device:TPU:25, one launch (start us, length us, event | category | flops | bytes accessed | tf_op | source)
XLA Modules:
  0.0 110.0 jit_solution(5626102418959281423)
XLA Ops:
  0.0 104.4 %fused.1 = (f32[12,1024,128]{2,1,0:T(8,128)}, f32[1024,128]{1,0:T(8,128)}) custom-call(f32[12]{0:T(128)} %skip1.1, f32[12]{0:T(128)} %skip2.1, bf16[4,256,1536]{2,1,0:T(8,128)(2,1)} %bitcast.4, bf16[4,256,1536]{2,1,0:T(8,128)(2,1)} %bitcast.5, bf16[256,4,1536]{2,1,0:T(4,128)(2,1)} %gate2_hbm.1, f32[12,1024]{1,0:T(8,128)} %refs_0_.1, f32[12,1024]{1,0:T(8,128)} %refs_1_.1, ...), custom_call_target="tpu_custom_call" | custom-call | tf_op jit(solution)/shard_map/fused/pallas_call | solution.py:782
  104.4 5.4 %norm.1 = bf16[256,4,1536]{2,1,0:T(4,128)(2,1)} custom-call(f32[12,1024,128]{2,1,0:T(8,128)} %get-tuple-element.7.gated_hbm, f32[1024,128]{1,0:T(8,128)} %get-tuple-element.8.scale_hbm, f32[12,128]{1,0:T(8,128)} %bitcast.7), custom_call_target="tpu_custom_call" | custom-call | tf_op jit(solution)/shard_map/norm/pallas_call | solution.py:823

commit v5 on v4

--- a/solution.py
+++ b/solution.py
@@ -184,22 +184,18 @@
     )
 
 
-def head_sum(count, own_ref, held, send_sems, recv_sems):
+def head_sum(count, own_ref, held, sems):
     me = lax.axis_index("head")
-    copies = []
+
+    def copy(source, target, hop):
+        return pltpu.make_async_remote_copy(
+            src_ref=source, dst_ref=target, send_sem=sems.at[0], recv_sem=sems.at[1],
+            device_id={"head": lax.rem(me + hop, count)}, device_id_type=MESH,
+        )
+
     for hop in range(1, count):
-        copy = pltpu.make_async_remote_copy(
-            src_ref=own_ref,
-            dst_ref=held.at[hop - 1],
-            send_sem=send_sems.at[hop - 1],
-            recv_sem=recv_sems.at[hop - 1],
-            device_id={"head": lax.rem(me + hop, count)},
-            device_id_type=MESH,
-        )
-        copy.start()
-        copies.append(copy)
-    for copy in copies:
-        copy.wait()
+        copy(own_ref, held.at[hop - 1], hop).start()
+    copy(held, held, 1).wait()
     total = own_ref[...]
     for hop in range(1, count):
         total += held[hop - 1]
@@ -213,6 +209,7 @@
         self.own, self.landed, self.pair_total, self.pair_totals, self.span = refs
         self.swap_sems, self.near_sems, self.pass_sems, self.own_sems, self.total_sems = sems
         self.seq, self.me = seq, lax.axis_index("seq")
+        self.chunks = self.swap_sems.shape[0] - 1
         me = lax.axis_index("seq")
         self.place = lax.rem(me, 2)
         self.partner = me + 1 - 2 * self.place
@@ -229,14 +226,14 @@
     def swap_copy(self, c, part):
         return pltpu.make_async_remote_copy(
             src_ref=self.sent.at[part], dst_ref=self.swapped.at[part],
-            send_sem=self.swap_sems.at[0, c], recv_sem=self.swap_sems.at[1, c],
+            send_sem=self.swap_sems.at[self.chunks], recv_sem=self.swap_sems.at[c],
             device_id={"seq": self.partner}, device_id_type=MESH,
         )
 
     def pass_copy(self, c, part):
         return pltpu.make_async_remote_copy(
             src_ref=self.passed.at[part], dst_ref=self.came.at[part],
-            send_sem=self.pass_sems.at[0, c], recv_sem=self.pass_sems.at[1, c],
+            send_sem=self.pass_sems.at[self.chunks], recv_sem=self.pass_sems.at[c],
             device_id={"seq": self.ahead}, device_id_type=MESH,
         )
 
@@ -255,7 +252,7 @@
         layer = self.layer
         first_fade, last_fade = fades
         even = self.place == 0
-        self.swap_copy(c, part).wait()
+        self.swap_copy(c, part).wait_recv()
 
         @pl.when(self.group > 0)
         def _():
@@ -300,7 +297,7 @@
         return jnp.where(even, mine, other), jnp.where(even, other, mine)
 
     def send_own(self, c, part, fades):
-        self.swap_copy(c, part).wait()
+        self.swap_copy(c, part).wait_recv()
         for i, h in enumerate(range(part.start, part.start + part.size)):
             first, last = self.pair_of(h)
             self.own[i] = (fades[1][h : h + 1] * first + last).astype(BF16)
@@ -332,12 +329,13 @@
             middle = fades[0][h : h + 1] * before + self.pair_of(h)[0]
             prior[h] = jnp.where(self.place == 0, before, middle)
 
-    def settle(self, parts):
-        for c, part in parts:
+    def settle(self, start, stop):
+        self.swap_copy(0, pl.ds(0, self.sent.shape[0])).wait_send()
+        if stop > start:
 
             @pl.when(self.group < self.groups - 1)
-            def _(c=c, part=part):
-                self.pass_copy(c, part).wait_send()
+            def _():
+                self.pass_copy(0, pl.ds(start, stop - start)).wait_send()
 
         for hop in range(1, self.groups):
 
@@ -352,7 +350,7 @@
     skip1, skip2, x_hbm, gate1_hbm, gate2_hbm, *refs
 ):
     small_hbm, refs = refs[:SMALL], refs[SMALL:]
-    out_hbm, scale_ref, x, gate1, gate2, sendbuf, recvbuf, hidden, innerbuf, turned, *refs = refs
+    out_hbm, total_ref, x, gate1, gate2, sendbuf, recvbuf, hidden, innerbuf, turned, *refs = refs
     small, refs = refs[:SMALL], refs[SMALL:]
     decay1, step1, write1, read1, gain1, decay2, step2, write2, read2 = small
     (
@@ -363,8 +361,7 @@
     ) = refs
     ex1_refs, ex2_refs, refs = refs[:10], refs[10:20], refs[20:]
     (
-        load_sems, small_sems, bulk_send, bulk_recv, keep_sems, sum1, sum2, scale_send, scale_recv,
-        out_sems, *refs,
+        load_sems, small_sems, bulk_sems, sum1, sum2, scale_sems, out_sem, *refs,
     ) = refs
     ex1_sems, ex2_sems = refs[:5], refs[5:]
     axes = (("seq", seq), ("head", head_count))
@@ -380,12 +377,12 @@
     greet_signal(axes)
 
     def load(b):
-        return pltpu.make_async_copy(x_hbm.at[b], x.at[b], load_sems.at[0, b])
+        return pltpu.make_async_copy(x_hbm.at[b], x.at[b], load_sems.at[b])
 
     gate_loads = [
-        pltpu.make_async_copy(gate1_hbm, gate1, load_sems.at[1, 0]),
+        pltpu.make_async_copy(gate1_hbm, gate1, load_sems.at[blocks]),
         pltpu.make_async_copy(
-            gate2_hbm, gate_raw if local_cols > 1 else gate2, load_sems.at[2, 0]
+            gate2_hbm, gate_raw if local_cols > 1 else gate2, load_sems.at[blocks + 1]
         ),
     ]
     small_loads = [
@@ -485,15 +482,15 @@
         return pltpu.make_async_remote_copy(
             src_ref=sendbuf.at[to, :, :, :, wide(c)],
             dst_ref=recvbuf.at[me, :, :, :, wide(c)],
-            send_sem=bulk_send.at[hop - 1, c],
-            recv_sem=bulk_recv.at[hop - 1, c],
+            send_sem=bulk_sems.at[0, c],
+            recv_sem=bulk_sems.at[1, c],
             device_id={"seq": to},
             device_id_type=MESH,
         )
 
     def keep(c):
         return pltpu.make_async_copy(
-            sendbuf.at[me, :, :, :, wide(c)], recvbuf.at[me, :, :, :, wide(c)], keep_sems.at[c]
+            sendbuf.at[me, :, :, :, wide(c)], recvbuf.at[me, :, :, :, wide(c)], bulk_sems.at[1, c]
         )
 
     def send_all(c):
@@ -515,7 +512,7 @@
         for c in range(1, chunks):
             ex1.step(c, parts[c], fades)
 
-    for hop in range(1, seq):
+    for hop in range(seq - 1, 0, -1):
 
         @pl.when(hop > me)
         def _(hop=hop):
@@ -533,21 +530,18 @@
         if c == 1:
             send_all(c)
     reduce_squares(one, rows1)
-    scale[...] = lax.rsqrt(head_sum(head_count, rows1, held1, sum1.at[0], sum1.at[1]) / inner + EPSILON)
+    scale[...] = lax.rsqrt(head_sum(head_count, rows1, held1, sum1) / inner + EPSILON)
     depth = scale.shape[0]
     mine = pl.ds(pl.multiple_of(me * depth, depth), depth)
-    scale_copies = []
+
+    def scale_copy(source, target, hop):
+        return pltpu.make_async_remote_copy(
+            src_ref=source, dst_ref=target, send_sem=scale_sems.at[0], recv_sem=scale_sems.at[1],
+            device_id={"seq": lax.rem(me - hop + seq, seq)}, device_id_type=MESH,
+        )
+
     for hop in range(1, seq):
-        copy = pltpu.make_async_remote_copy(
-            src_ref=scale,
-            dst_ref=scales.at[mine],
-            send_sem=scale_send.at[hop - 1],
-            recv_sem=scale_recv.at[hop - 1],
-            device_id={"seq": lax.rem(me - hop + seq, seq)},
-            device_id_type=MESH,
-        )
-        copy.start()
-        scale_copies.append(copy)
+        scale_copy(scale, scales.at[mine], hop).start()
     for c in range(2, chunks):
         send_all(c)
     scales[mine, :] = scale[...]
@@ -569,7 +563,7 @@
 
     if local_cols > 1:
         for h in range(heads):
-            slot = woven.at[h % 2]
+            slot = woven.at[h % CHUNK]
             slot[...] = gate_raw[:, :, lanes_of(h)].astype(F32).reshape(all_rows * local_cols, LANES)
             for b in range(blocks):
                 at = (b % per_col) * BLOCK * local_cols + b // per_col
@@ -578,8 +572,8 @@
         for h in range(heads):
             for b in range(blocks):
                 silus[b, :, lanes_of(h)] = silu(gate2[b, :, lanes_of(h)])
-    for copy in scale_copies:
-        copy.wait()
+    others = scales.at[pl.ds(0, (seq - 1) * depth)]
+    scale_copy(others, others, 1).wait()
 
     def columns(b, carry):
         window = pl.ds(
@@ -591,10 +585,19 @@
 
     lax.fori_loop(0, blocks, columns, 0)
 
+    def bulk_all(c, count):
+        some = pl.ds(0, count)
+        return pltpu.make_async_remote_copy(
+            src_ref=sendbuf.at[some, :, :, :, wide(c)],
+            dst_ref=recvbuf.at[some, :, :, :, wide(c)],
+            send_sem=bulk_sems.at[0, c],
+            recv_sem=bulk_sems.at[1, c],
+            device_id={"seq": lax.rem(me + 1, seq)},
+            device_id_type=MESH,
+        )
+
     def arrive(c):
-        keep(c).wait()
-        for hop in range(1, seq):
-            bulk(c, hop).wait()
+        bulk_all(c, seq).wait_recv()
 
     def states2(c):
         def block(b, carry):
@@ -619,10 +622,10 @@
         lax.fori_loop(0, blocks, block, 0)
 
     def store2(b, h, gated):
-        flat[h, place_of(b), :] = gated
+        woven[h % CHUNK, place_of(b), :] = gated
 
     def put(c):
-        return pltpu.make_async_copy(flat.at[parts[c]], out_hbm.at[parts[c]], out_sems.at[c])
+        return pltpu.make_async_copy(flat.at[parts[c]], out_hbm.at[parts[c]], out_sem.at[0])
 
     def finish2(c):
         def block(b, carry):
@@ -630,10 +633,13 @@
             return carry
 
         lax.fori_loop(0, blocks, block, 0)
+        for h in numbers[c]:
+            flat[h] = woven[h % CHUNK].astype(BF16)
         put(c).start()
 
     last = chunks - 1
     fades = ex2_fades
+    ends = ex2.group == ex2.groups - 1
 
     def chain(slot):
         for late in range(2):
@@ -658,16 +664,16 @@
         arrive(c)
         states2(c)
         ex2.swap(c, parts[c])
+        if c == last:
+
+            @pl.when(jnp.logical_not(soon | ends))
+            def _():
+                for e in range(last):
+                    ex2.step(e, parts[e], fades)
+
         inner2(c)
         if c < last:
             chain(c)
-    ends = ex2.group == ex2.groups - 1
-
-    @pl.when(jnp.logical_not(soon | ends))
-    def _():
-        for e in range(last):
-            ex2.step(e, parts[e], fades)
-
     ex2.send_own(last, parts[last], fades)
     for e in range(last):
 
@@ -686,33 +692,31 @@
     ex2.take_own(parts[last], fades)
     finish2(last)
     reduce_squares(two, rows1)
-    total = head_sum(head_count, rows1, held2, sum2.at[0], sum2.at[1])
-    total = jnp.transpose(lax.rsqrt(total / inner + EPSILON))
-    for b in range(blocks):
-        at = (b % per_col) * BLOCK * local_cols + b // per_col
-        scale_ref[pl.ds(at, BLOCK, stride=local_cols), :] = jnp.broadcast_to(
-            total[:, b : b + 1], (BLOCK, LANES)
-        )
+    total_ref[...] = head_sum(head_count, rows1, held2, sum2)
+    pltpu.make_async_copy(flat, out_hbm, out_sem.at[0]).wait()
     for c in range(chunks):
-        put(c).wait()
-    numbered = list(enumerate(parts))
-    ex1.settle(numbered[1:])
-    ex2.settle(numbered[:-1])
-
-
-def norm_kernel(steps, gated_hbm, scale_hbm, gain_ref, out_hbm, gated, scale, out, load_sems, out_sems):
+        bulk_all(c, seq - 1).wait_send()
+    ex1.settle(numbers[0][-1] + 1, heads)
+    ex2.settle(0, numbers[last][0])
+
+
+def norm_kernel(
+    steps, inner, per_col, gated_hbm, total_hbm, gain_hbm, out_hbm, gated, total, gain, scale, out,
+    load_sems, out_sems,
+):
     heads, rows, _ = gated.shape
     part = rows // steps
     tall = out.shape[0] // steps
+    local_cols = rows // (per_col * BLOCK)
+    small = [
+        pltpu.make_async_copy(total_hbm, total, load_sems.at[steps]),
+        pltpu.make_async_copy(gain_hbm, gain, load_sems.at[steps + 1]),
+    ]
     loads = [
-        pltpu.make_async_copy(scale_hbm, scale, load_sems.at[steps]),
-        *(
-            pltpu.make_async_copy(
-                gated_hbm.at[:, pl.ds(i * part, part)], gated.at[:, pl.ds(i * part, part)],
-                load_sems.at[i],
-            )
-            for i in range(steps)
-        ),
+        pltpu.make_async_copy(
+            gated_hbm.at[:, pl.ds(i * part, part)], gated.at[:, pl.ds(i * part, part)], load_sems.at[i]
+        )
+        for i in range(steps)
     ]
     puts = [
         pltpu.make_async_copy(
@@ -720,17 +724,23 @@
         )
         for i in range(steps)
     ]
-    for copy in loads:
+    for copy in small + loads:
         copy.start()
-    loads[0].wait()
+    for copy in small:
+        copy.wait()
+    columns = jnp.transpose(lax.rsqrt(total[...] / inner + EPSILON))
+    for b in range(rows // BLOCK):
+        at = (b % per_col) * BLOCK * local_cols + b // per_col
+        scale[pl.ds(at, BLOCK, stride=local_cols), :] = jnp.broadcast_to(
+            columns[:, b : b + 1], (BLOCK, LANES)
+        )
     for i in range(steps):
-        loads[i + 1].wait()
+        loads[i].wait()
         span = pl.ds(i * part, part)
         for h in range(heads):
-            lanes = lanes_of(h)
-            result = gated[h, span, :] * scale[span, :] * gain_ref[h : h + 1, :]
+            result = gated[h, span, :].astype(F32) * scale[span, :] * gain[h : h + 1, :]
             shape = (tall,) + out.shape[1:-1] + (LANES,)
-            out[pl.ds(i * tall, tall), ..., lanes] = result.reshape(shape).astype(BF16)
+            out[pl.ds(i * tall, tall), ..., lanes_of(h)] = result.reshape(shape).astype(BF16)
         puts[i].start()
     for copy in puts:
         copy.wait()
@@ -771,7 +781,7 @@
         vmem(total, F32), vmem(held, BF16), vmem((far,) + held, BF16), vmem(total, F32),
         vmem((far,) + total, F32), vmem(total, F32),
     ]
-    exchange_sems = [dma((2, chunks)), dma((2,)), dma((2, chunks)), dma((2, far)), dma((2, far))]
+    exchange_sems = [dma((chunks + 1,)), dma((2,)), dma((chunks + 1,)), dma((2, far)), dma((2, far))]
     small = (
         decay_rows, step_rows, write_rows, read_rows, norm_rows.reshape(heads, width),
         decay_cols, step_cols, write_cols, read_cols,
@@ -779,11 +789,11 @@
     raw = (all_rows, local_cols, features)
     flat = raw if local_cols > 1 else (all_rows, features)
     gate = gate_cols if local_cols > 1 else gate_cols.reshape(tokens)
-    gated, scale = pl.pallas_call(
+    gated, squares = pl.pallas_call(
         functools.partial(fused_kernel, seq, head, inner, grid_cols, local_cols, per_col),
         out_shape=(
-            jax.ShapeDtypeStruct((heads, all_rows * local_cols, LANES), F32),
-            jax.ShapeDtypeStruct((all_rows * local_cols, LANES), F32),
+            jax.ShapeDtypeStruct((heads, all_rows * local_cols, LANES), BF16),
+            jax.ShapeDtypeStruct((depth, BLOCK), F32),
         ),
         in_specs=[smem, smem] + [anywhere] * (3 + SMALL),
         out_specs=(anywhere, whole),
@@ -794,8 +804,8 @@
             vmem(tokens, F32), vmem((2, BLOCK, LANES), F32),
             *(vmem(array.shape, array.dtype) for array in small),
             vmem(raw if local_cols > 1 else (1, LANES), BF16),
-            vmem((heads, all_rows * local_cols, LANES), F32),
-            vmem((2, all_rows * local_cols if local_cols > 1 else 8, LANES), F32),
+            vmem((heads, all_rows * local_cols, LANES), BF16),
+            vmem((CHUNK, all_rows * local_cols, LANES), F32),
             vmem(tokens, F32),
             vmem((blocks, 3, padded, BLOCK), BF16), vmem(sums, F32), vmem(sums, F32),
             vmem(sums, F32), vmem(rows, F32), vmem(rows, F32), vmem(rows, F32), vmem(rows, F32),
@@ -807,9 +817,9 @@
             vmem((depth, BLOCK), F32), vmem((seq * depth, BLOCK), F32),
             vmem((blocks, BLOCK, LANES), F32),
             *exchange, *exchange,
-            dma((3, blocks)), dma((SMALL,)), dma((seq - 1, chunks)), dma((seq - 1, chunks)), dma((chunks,)),
-            dma((2, head - 1)), dma((2, head - 1)), dma((seq - 1,)), dma((seq - 1,)),
-            dma((chunks,)),
+            dma((blocks + 2,)), dma((SMALL,)), dma((2, chunks)),
+            dma((2,)), dma((2,)), dma((2,)),
+            dma((1,)),
             *exchange_sems, *exchange_sems,
         ],
         compiler_params=pltpu.CompilerParams(
@@ -821,17 +831,18 @@
     )
     steps = 8
     result = pl.pallas_call(
-        functools.partial(norm_kernel, steps),
+        functools.partial(norm_kernel, steps, inner, per_col),
         out_shape=jax.ShapeDtypeStruct(flat, BF16),
-        in_specs=[anywhere, anywhere, whole],
+        in_specs=[anywhere] * 3,
         out_specs=anywhere,
         scratch_shapes=[
-            vmem(gated.shape, F32), vmem(scale.shape, F32), vmem(flat, BF16),
-            dma((steps + 1,)), dma((steps,)),
+            vmem(gated.shape, BF16), vmem(squares.shape, F32), vmem((heads, width), F32),
+            vmem((all_rows * local_cols, LANES), F32), vmem(flat, BF16),
+            dma((steps + 2,)), dma((steps,)),
         ],
         compiler_params=pltpu.CompilerParams(vmem_limit_bytes=VMEM_BYTES),
         name="norm",
-    )(gated, scale, norm_cols.reshape(heads, width))
+    )(gated, squares, norm_cols.reshape(heads, width))
     return result.reshape(all_rows, local_cols, features)
 
 

time: 110 us -> 106 us (0.964)
  Pallas kernels: 110 us -> 106 us
    pallas_call x1, Pallas kernels: 104 us -> 102 us  [body(): pl.pallas_call(functools.partial(fused_kernel, seq, head, inner, grid_col...]
    pallas_call x1, Pallas kernels: 5.39 us -> 3.25 us  [body(): pl.pallas_call(functools.partial(norm_kernel, steps, inner, per_col), out...]
where the time goes in v5:
time: 106 us
  Pallas kernels  106 us (100%)
    pallas_call x1, Pallas kernels, body(): pl.pallas_call(functools.partial(fused_kernel, seq, head, inner, grid_col...  102 us
    pallas_call x1, Pallas kernels, body(): pl.pallas_call(functools.partial(norm_kernel, steps, inner, per_col), out...  3.25 us

profile of v5, /device:TPU:25, one launch (start us, length us, event | category | flops | bytes accessed | tf_op | source)
XLA Modules:
  0.0 105.7 jit_solution(13550887530156956059)
XLA Ops:
  0.0 102.3 %fused.1 = (bf16[12,1024,128]{2,1,0:T(8,128)(2,1)}, f32[8,256]{1,0:T(8,128)}) custom-call(f32[12]{0:T(128)} %skip1.1, f32[12]{0:T(128)} %skip2.1, bf16[4,256,1536]{2,1,0:T(8,128)(2,1)} %bitcast.4, bf16[4,256,1536]{2,1,0:T(8,128)(2,1)} %bitcast.5, bf16[256,4,1536]{2,1,0:T(4,128)(2,1)} %gate2_hbm.1, f32[12,1024]{1,0:T(8,128)} %refs_0_.1, f32[12,1024]{1,0:T(8,128)} %refs_1_.1, ...), custom_call_target="tpu_custom_call" | custom-call | tf_op jit(solution)/shard_map/fused/pallas_call | solution.py:792
  102.3 3.3 %norm.1 = bf16[256,4,1536]{2,1,0:T(4,128)(2,1)} custom-call(bf16[12,1024,128]{2,1,0:T(8,128)(2,1)} %get-tuple-element.7.gated_hbm, f32[8,256]{1,0:T(8,128)} %get-tuple-element.8.total_hbm, f32[12,128]{1,0:T(8,128)} %bitcast.7), custom_call_target="tpu_custom_call" | custom-call | tf_op jit(solution)/shard_map/norm/pallas_call | solution.py:833

commit v6 on v5

--- a/solution.py
+++ b/solution.py
@@ -121,10 +121,13 @@
 
     skip = layer.skip[h]
     first = contract(mix(top, top, True), own[top], ((1,), (0,)))
-    layer.inner[b, top, lanes_of(h)] = first + skip * own[top].astype(F32)
+    lanes = lanes_of(h)
+    gate = layer.silu[b, :, lanes]
+    layer.silu[b, :, lanes] = gate * layer.lifting[b, :, h : h + 1]
+    layer.inner[b, top, lanes] = (first + skip * own[top].astype(F32)) * gate[top]
     both = jnp.concatenate([mix(low, top, False), mix(low, low, True)], axis=1)
     second = contract(both, own, ((1,), (0,)))
-    layer.inner[b, low, lanes_of(h)] = second + skip * own[low].astype(F32)
+    layer.inner[b, low, lanes] = (second + skip * own[low].astype(F32)) * gate[low]
 
 
 def finish_block(layer, b, hs, store):
@@ -135,9 +138,9 @@
     from_state = contract(layer.read_t[b], parts, ((1,), (0,)))
     squares = jnp.zeros((BLOCK, LANES), F32)
     for i, h in enumerate(hs):
-        out = layer.inner[b, :, lanes_of(h)]
-        out += layer.lifting[b, :, h : h + 1] * from_state[:, i * LANES : (i + 1) * LANES]
-        gated = out * layer.silu[b, :, lanes_of(h)]
+        lanes = lanes_of(h)
+        gated = layer.silu[b, :, lanes] * from_state[:, i * LANES : (i + 1) * LANES]
+        gated += layer.inner[b, :, lanes]
         squares += gated * gated
         store(b, h, gated)
     layer.squares[b] += squares
@@ -434,8 +437,8 @@
     def inner1(c):
         def block(b, carry):
             for h in numbers[c]:
+                silus[b, :, lanes_of(h)] = silu(gate1[b, :, lanes_of(h)])
                 inner_block(one, b, h, x[b, :, lanes_of(h)])
-                silus[b, :, lanes_of(h)] = silu(gate1[b, :, lanes_of(h)])
             return carry
 
         lax.fori_loop(0, blocks, block, 0)
@@ -632,7 +635,7 @@
             finish_block(two, b, numbers[c], store2)
             return carry
 
-        lax.fori_loop(0, blocks, block, 0)
+        lax.fori_loop(0, blocks, block, 0, unroll=True)
         for h in numbers[c]:
             flat[h] = woven[h % CHUNK].astype(BF16)
         put(c).start()

time: 106 us -> 104 us (0.981)
  Pallas kernels: 106 us -> 103 us
    pallas_call x1, Pallas kernels: 102 us -> 100 us  [body(): pl.pallas_call(functools.partial(fused_kernel, seq, head, inner, grid_col...]
where the time goes in v6:
time: 104 us
  Pallas kernels  103 us (99%)
    pallas_call x1, Pallas kernels, body(): pl.pallas_call(functools.partial(fused_kernel, seq, head, inner, grid_col...  100 us
    pallas_call x1, Pallas kernels, body(): pl.pallas_call(functools.partial(norm_kernel, steps, inner, per_col), out...  3.25 us

profile of v6, /device:TPU:25, one launch (start us, length us, event | category | flops | bytes accessed | tf_op | source)
XLA Modules:
  0.0 103.5 jit_solution(16825440374695722173)
XLA Ops:
  0.0 100.1 %fused.1 = (bf16[12,1024,128]{2,1,0:T(8,128)(2,1)}, f32[8,256]{1,0:T(8,128)}) custom-call(f32[12]{0:T(128)} %skip1.1, f32[12]{0:T(128)} %skip2.1, bf16[4,256,1536]{2,1,0:T(8,128)(2,1)} %bitcast.4, bf16[4,256,1536]{2,1,0:T(8,128)(2,1)} %bitcast.5, bf16[256,4,1536]{2,1,0:T(4,128)(2,1)} %gate2_hbm.1, f32[12,1024]{1,0:T(8,128)} %refs_0_.1, f32[12,1024]{1,0:T(8,128)} %refs_1_.1, ...), custom_call_target="tpu_custom_call" | custom-call | tf_op jit(solution)/shard_map/fused/pallas_call | solution.py:795
  100.1 3.3 %norm.1 = bf16[256,4,1536]{2,1,0:T(4,128)(2,1)} custom-call(bf16[12,1024,128]{2,1,0:T(8,128)(2,1)} %get-tuple-element.7.gated_hbm, f32[8,256]{1,0:T(8,128)} %get-tuple-element.8.total_hbm, f32[12,128]{1,0:T(8,128)} %bitcast.7), custom_call_target="tpu_custom_call" | custom-call | tf_op jit(solution)/shard_map/norm/pallas_call | solution.py:836

commit v7 on v6

--- a/solution.py
+++ b/solution.py
@@ -446,12 +446,12 @@
     small_loads[3].wait()
     prepare_scores(one)
     squares[...] = jnp.zeros_like(squares)
-    gate_loads[0].wait()
-    inner1(0)
     greet_wait(axes)
     ex1.near_copy().start()
     for c, part in enumerate(parts):
         ex1.swap(c, part)
+    gate_loads[0].wait()
+    inner1(0)
     fades = ex1.fades()
     ex1.announce()
     ex1.send_own(0, parts[0], fades)

time: 104 us -> 103 us (level)
  no operation moved by 1% of the time
where the time goes in v7:
time: 103 us
  Pallas kernels  103 us (100%)
    pallas_call x1, Pallas kernels, body(): pl.pallas_call(functools.partial(fused_kernel, seq, head, inner, grid_col...  99.5 us
    pallas_call x1, Pallas kernels, body(): pl.pallas_call(functools.partial(norm_kernel, steps, inner, per_col), out...  3.25 us

profile of v7, /device:TPU:25, one launch (start us, length us, event | category | flops | bytes accessed | tf_op | source)
XLA Modules:
  0.0 102.9 jit_solution(6435321399154222415)
XLA Ops:
  0.0 99.5 %fused.1 = (bf16[12,1024,128]{2,1,0:T(8,128)(2,1)}, f32[8,256]{1,0:T(8,128)}) custom-call(f32[12]{0:T(128)} %skip1.1, f32[12]{0:T(128)} %skip2.1, bf16[4,256,1536]{2,1,0:T(8,128)(2,1)} %bitcast.4, bf16[4,256,1536]{2,1,0:T(8,128)(2,1)} %bitcast.5, bf16[256,4,1536]{2,1,0:T(4,128)(2,1)} %gate2_hbm.1, f32[12,1024]{1,0:T(8,128)} %refs_0_.1, f32[12,1024]{1,0:T(8,128)} %refs_1_.1, ...), custom_call_target="tpu_custom_call" | custom-call | tf_op jit(solution)/shard_map/fused/pallas_call | solution.py:795
  99.5 3.3 %norm.1 = bf16[256,4,1536]{2,1,0:T(4,128)(2,1)} custom-call(bf16[12,1024,128]{2,1,0:T(8,128)(2,1)} %get-tuple-element.7.gated_hbm, f32[8,256]{1,0:T(8,128)} %get-tuple-element.8.total_hbm, f32[12,128]{1,0:T(8,128)} %bitcast.7), custom_call_target="tpu_custom_call" | custom-call | tf_op jit(solution)/shard_map/norm/pallas_call | solution.py:836

commit v8 on v7

--- a/solution.py
+++ b/solution.py
@@ -441,7 +441,7 @@
                 inner_block(one, b, h, x[b, :, lanes_of(h)])
             return carry
 
-        lax.fori_loop(0, blocks, block, 0)
+        lax.fori_loop(0, blocks, block, 0, unroll=2)
 
     small_loads[3].wait()
     prepare_scores(one)
@@ -622,7 +622,7 @@
                 inner_block(two, b, h, hidden[b, :, lanes_of(h)])
             return carry
 
-        lax.fori_loop(0, blocks, block, 0)
+        lax.fori_loop(0, blocks, block, 0, unroll=2)
 
     def store2(b, h, gated):
         woven[h % CHUNK, place_of(b), :] = gated

time: 103 us -> 103 us (level)
  no operation moved by 1% of the time
where the time goes in v8:
time: 103 us; the launch traced here: 102 us
  Pallas kernels  102 us (99%)
    pallas_call x1, Pallas kernels, body(): pl.pallas_call(functools.partial(fused_kernel, seq, head, inner, grid_col...  99 us
    pallas_call x1, Pallas kernels, body(): pl.pallas_call(functools.partial(norm_kernel, steps, inner, per_col), out...  3.25 us

profile of v8, /device:TPU:25, one launch (start us, length us, event | category | flops | bytes accessed | tf_op | source)
XLA Modules:
  0.0 102.4 jit_solution(7673455516497934741)
XLA Ops:
  0.0 99.0 %fused.1 = (bf16[12,1024,128]{2,1,0:T(8,128)(2,1)}, f32[8,256]{1,0:T(8,128)}) custom-call(f32[12]{0:T(128)} %skip1.1, f32[12]{0:T(128)} %skip2.1, bf16[4,256,1536]{2,1,0:T(8,128)(2,1)} %bitcast.4, bf16[4,256,1536]{2,1,0:T(8,128)(2,1)} %bitcast.5, bf16[256,4,1536]{2,1,0:T(4,128)(2,1)} %gate2_hbm.1, f32[12,1024]{1,0:T(8,128)} %refs_0_.1, f32[12,1024]{1,0:T(8,128)} %refs_1_.1, ...), custom_call_target="tpu_custom_call" | custom-call | tf_op jit(solution)/shard_map/fused/pallas_call | solution.py:795
  99.0 3.3 %norm.1 = bf16[256,4,1536]{2,1,0:T(4,128)(2,1)} custom-call(bf16[12,1024,128]{2,1,0:T(8,128)(2,1)} %get-tuple-element.7.gated_hbm, f32[8,256]{1,0:T(8,128)} %get-tuple-element.8.total_hbm, f32[12,128]{1,0:T(8,128)} %bitcast.7), custom_call_target="tpu_custom_call" | custom-call | tf_op jit(solution)/shard_map/norm/pallas_call | solution.py:836
